TPU v7x, 512 devices: a whole 4x8x8 slice. The times are simulated.
512 devices in a mesh: blk: 32 (over y, z_lo), group: 16 (over z_hi, x, core).
Axes of the slice: x: 4, y: 8, z: 8 (z_hi: 2, z_lo: 4; z = z_hi * 4 + z_lo), core: 2. Of those that a mesh axis runs over, the one named last changes fastest.
Arguments:
- vertex_matrix: bfloat16 [512, 1152, 1152], P(('blk', 'group')), may hold values from -0.1875 to 0.1875
- vertex_site: int32 [512, 1152], P(('blk', 'group')), may hold values from 0 to 15
- vertex_time: int32 [512, 1152], P(('blk', 'group')), may hold values from 0 to 1023
- vertex_spin: int32 [512, 1152], P(('blk', 'group')), may hold values from 0 to 1
- free_green: float32 [2, 128], replicated, may hold values from -3 to 3
- plus_table: int32 [128, 128], replicated, may hold values from 0 to 127, each once within a row
- cross_table: int32 [128, 128], P('blk'), may hold values from 0 to 127, each once within a row
Outputs:
- crossed: float32 [2, 128, 128, 128], P(None, 'blk', None, 'group')
Inputs may be any that keep to these rules, and one draw needn't show every extreme that they name: `plus_table`: each row is a permutation of 0 to 127. `cross_table`: each row is a permutation of 0 to 127.
All inputs are finite; a program needn't handle non-finite values.
Results may differ from a plain program's by a relative error of at most 0.0078.
Values may be sent and summed in bfloat16 or wider, within the bound.
No kernel may reach another device: no remote copies, remote signals or barrier semaphores. Data moves between devices by JAX's collectives and lax.ppermute only.
A program may use at most 64 MiB of HBM per device.

v0:
```python
import math

import jax
import jax.numpy as jnp
from jax import lax
from jax.sharding import PartitionSpec as P

LX = 4
NW = 8
W = 128
NV = 1152
NT = 1024


def sent_together(arrays, axis, dim, along):
    widths = [a.shape[along] for a in arrays]
    both = jnp.concatenate(arrays, axis=along)
    out = lax.all_gather(both, axis, axis=dim, tiled=True)
    return tuple(jnp.split(out, [sum(widths[:k]) for k in range(1, len(widths))], axis=along))


def in_blocks(value, dim, devices):
    before, after = (value.shape[:dim], value.shape[dim + 1 :])
    return jnp.moveaxis(value.reshape(*before, devices, -1, *after), dim, 0)


def sent_and_summed(value, axis, dim):
    devices = lax.axis_size(axis)
    parts = lax.all_to_all(in_blocks(value, dim, devices), axis, 0, 0, tiled=True)
    return jnp.sum(parts, axis=0)


def phases(site_ids, time_ids):
    points = jnp.arange(W, dtype=jnp.int32)
    moment = points // NW
    freq_index = points % NW
    kx_part = moment % LX
    ky_part = moment // LX
    rx_part = site_ids % LX
    ry_part = site_ids // LX
    winding = (2 * freq_index + 1)[:, None] * time_ids[None, :] + 2 * NT // LX * (
        kx_part[:, None] * rx_part[None, :] + ky_part[:, None] * ry_part[None, :]
    )
    winding = winding % (2 * NT)
    return winding.astype(jnp.float32) * (math.pi / NT)


def green_pair(matrix, site_ids, time_ids, spin_ids, free_green):
    angles = phases(site_ids, time_ids)
    cosine = jnp.cos(angles)
    sine_part = jnp.sin(angles)
    spin_up = (spin_ids == 0).astype(jnp.float32)[None, :]
    spin_down = (spin_ids == 1).astype(jnp.float32)[None, :]
    fourier_rows = jnp.concatenate(
        [cosine * spin_up, sine_part * spin_up, cosine * spin_down, sine_part * spin_down], 0
    ).astype(jnp.bfloat16)
    projected = jnp.dot(fourier_rows, matrix, preferred_element_type=jnp.float32).astype(
        jnp.bfloat16
    )
    norm_factor = 1.0 / math.sqrt(NV)
    real_free = free_green[0]
    imag_free = free_green[1]
    greens = []
    for spin_index in range(2):
        offset = 2 * W * spin_index
        cosine_rows = fourier_rows[offset : offset + W]
        sine_rows = fourier_rows[offset + W : offset + 2 * W]
        proj_real = projected[offset : offset + W]
        proj_imag = projected[offset + W : offset + 2 * W]
        left_block = jnp.concatenate(
            [
                jnp.concatenate([proj_real, proj_imag], 1),
                jnp.concatenate([proj_imag, -proj_real], 1),
            ],
            0,
        )
        right_block = jnp.concatenate([cosine_rows, sine_rows], 1)
        kernel = lax.dot_general(
            left_block, right_block, (((1,), (1,)), ((), ())), preferred_element_type=jnp.float32
        )
        kernel_real = kernel[:W]
        kernel_imag = kernel[W:]
        half_real = real_free[:, None] * kernel_real - imag_free[:, None] * kernel_imag
        half_imag = real_free[:, None] * kernel_imag + imag_free[:, None] * kernel_real
        green_real = (
            -(half_real * real_free[None, :] - half_imag * imag_free[None, :]) * norm_factor
        )
        green_imag = (
            -(half_real * imag_free[None, :] + half_imag * real_free[None, :]) * norm_factor
        )
        greens.append(jnp.stack([green_real, green_imag], 0))
    green_sum = (greens[0] + greens[1]).astype(jnp.bfloat16)
    return (green_sum, greens[0].astype(jnp.bfloat16), greens[1].astype(jnp.bfloat16))


def direct_terms(sums_piece, perm_row):
    column_ids = jnp.arange(sums_piece.shape[-1], dtype=jnp.int32)
    selector = (perm_row[:, None] == column_ids[None, :]).astype(jnp.bfloat16)
    halfway = jnp.einsum(
        "aj,kcbj->kcab", selector, sums_piece, preferred_element_type=jnp.float32
    ).astype(jnp.bfloat16)
    partner = jnp.einsum("kcaj,bj->kcab", halfway, selector, preferred_element_type=jnp.float32)
    local_copy = sums_piece.astype(jnp.float32)
    real_part = jnp.sum(local_copy[:, 0] * partner[:, 0] - local_copy[:, 1] * partner[:, 1], axis=0)
    imag_part = jnp.sum(local_copy[:, 0] * partner[:, 1] + local_copy[:, 1] * partner[:, 0], axis=0)
    return jnp.stack([real_part, imag_part], 0)


def copy_exchange(up_piece, down_piece, perm_row):
    column_ids = jnp.arange(up_piece.shape[-1], dtype=jnp.int32)
    spin_pieces = jnp.concatenate([up_piece, down_piece], 0)
    lead_values = spin_pieces[:, :, column_ids, perm_row]
    trail_values = spin_pieces[:, :, perm_row, column_ids]
    real_part = jnp.einsum(
        "ka,kb->ab", lead_values[:, 0], trail_values[:, 0], preferred_element_type=jnp.float32
    ) - jnp.einsum(
        "ka,kb->ab", lead_values[:, 1], trail_values[:, 1], preferred_element_type=jnp.float32
    )
    imag_part = jnp.einsum(
        "ka,kb->ab", lead_values[:, 0], trail_values[:, 1], preferred_element_type=jnp.float32
    ) + jnp.einsum(
        "ka,kb->ab", lead_values[:, 1], trail_values[:, 0], preferred_element_type=jnp.float32
    )
    return jnp.stack([real_part, imag_part], 0)


def body(vertex_matrix, vertex_site, vertex_time, vertex_spin, free_green, plus_table, cross_table):
    green_sum, green_up, green_down = green_pair(
        vertex_matrix[0], vertex_site[0], vertex_time[0], vertex_spin[0], free_green
    )
    slices = plus_table.shape[0] // lax.axis_size("blk")
    owned_perms = lax.dynamic_slice_in_dim(plus_table, lax.axis_index("blk") * slices, slices, 0)
    sums_piece, up_piece, down_piece = sent_together(
        (green_sum[None], green_up[None], green_down[None]), "blk", 0, 1
    )

    def one_slice(perm_row):
        return direct_terms(sums_piece, perm_row) - copy_exchange(up_piece, down_piece, perm_row)

    transfer = jnp.swapaxes(lax.map(one_slice, owned_perms), 0, 1)
    shares = sent_and_summed(transfer, "group", 3)
    regrouped = lax.all_to_all(shares, "blk", split_axis=2, concat_axis=1, tiled=True)
    row_ids = jnp.arange(regrouped.shape[2], dtype=jnp.int32)
    return regrouped[:, cross_table, row_ids[:, None], :]


def solution(mesh):
    in_specs = (
        P(("blk", "group"), None, None),
        P(("blk", "group"), None),
        P(("blk", "group"), None),
        P(("blk", "group"), None),
        P(),
        P(),
        P("blk", None),
    )
    out_specs = P(None, "blk", None, "group")
    return jax.shard_map(body, mesh=mesh, in_specs=in_specs, out_specs=out_specs, check_vma=False)
```

profile of v0, /device:TPU:1, one launch (start us, length us, event | category | flops | bytes accessed | tf_op | source)
XLA Modules:
  0.0 348.9 jit_solution(15056596487299832598)
XLA Ops:
  6.6 0.9 slice_bitcast_fusion.1
  7.4 0.7 fusion.62
  8.1 0.7 fusion.61
  8.9 0.7 reduce.2
  9.6 2.8 multiply_convert_fusion.3
  12.4 1.9 convolution_convert_fusion
  15.6 0.7 pad_maximum_fusion.1
  16.3 0.7 constant_dynamic-slice_fusion.1
  17.0 151.1 %all-gather.2.cloned.1.call-done = bf16[32,6,128,128]{3,2,1,0:T(8,128)(2,1)} async-done(((bf16[1,6,128,128]{3,2,1,0:T(8,128)(2,1)}), bf16[32,6,128,128]{3,2,1,0:T(8,128)(2,1)}) %all-gather.2.cloned.1.call-update) | async-done | bytes 6291472 | tf_op jit(solution)/shard_map/all_gather | solution.py:18
  168.1 6.9 %fusion.78 = (bf16[32,2,128,128]{3,2,1,0:T(8,128)(2,1)S(1)}, bf16[32,2,128,128]{3,2,1,0:T(8,128)(2,1)S(1)}, bf16[32,2,128,128]{3,2,1,0:T(8,128)(2,1)}) fusion(bf16[32,6,128,128]{3,2,1,0:T(8,128)(2,1)} %all-gather.2.cloned.1.call-done), kind=kLoop, calls=%fused_computation.132 | loop fusion | bytes 12582912 | tf_op jit(solution)/shard_map/split | solution.py:19
  175.0 2.3 pad_maximum_fusion
  177.3 14.4 %copy.31 = bf16[64,2,128,128]{0,1,3,2:T(2,128)(2,1)} copy(bf16[64,2,128,128]{3,2,1,0:T(8,128)(2,1)} %pad_maximum_fusion) | data formatting | bytes 8388608 | tf_op jit(solution)/shard_map/while | solution.py:140
  191.7 77.5 %while.12 = (s32[]{:T(128)}, f32[4,2,128,128]{2,3,0,1:T(8,128)}, bf16[32,2,128,128]{3,2,1,0:T(8,128)(2,1)}, s32[4,128]{1,0:T(4,128)S(1)}, bf16[64,2,128,128]{0,1,3,2:T(2,128)(2,1)}, /*index=5*/s32[]{:T(128)}) while((s32[]{:T(128)}, f32[4,2,128,128]{2,3,0,1:T(8,128)}, bf16[32,2,128,128]{3,2,1,0:T(8,128)(2,1)}, s32[4,128]{1,0:T(4,128)S(1)}, ...), condition=%wide.region_3.4_spmd, body=%wide.region_0.3_spmd.sunk | while | flops 551683584 | bytes 39721076 | solution.py:140
  191.7 4.9 %fusion.114 = f32[32,2,128,128]{3,2,1,0:T(8,128)} fusion(bf16[32,2,128,128]{3,2,1,0:T(8,128)(2,1)} %get-tuple-element.198, s32[128]{0:T(128)S(1)} %fusion.113), kind=kOutput, calls=%fused_computation.3.clone.1 | convolution fusion | flops 537952256 | bytes 6291968 | tf_op jit(solution)/shard_map/while/body/eval_jaxpr/kcaj,bj->kcab/dot_general | solution.py:102
  196.6 2.3 convert_element_type.86
  199.4 1.0 subtract_reduce_fusion.2
  200.4 4.3 %gather_fusion = bf16[128,64,2]{1,2,0:T(2,128)(2,1)S(1)} fusion(bf16[64,2,128,128]{0,1,3,2:T(2,128)(2,1)} %get-tuple-element.200, s32[128]{0:T(128)S(1)} %or_bitcast_fusion.5), kind=kCustom, calls=%fused_computation.1.clone.1 | custom fusion | bytes 66560 | tf_op jit(solution)/shard_map/while/body/eval_jaxpr/gather | solution.py:113
  204.9 4.3 %gather_fusion.1 = bf16[128,64,2]{1,2,0:T(2,128)(2,1)S(1)} fusion(bf16[64,2,128,128]{0,1,3,2:T(2,128)(2,1)} %get-tuple-element.200, s32[128]{0:T(128)S(1)} %get-tuple-element.180), kind=kCustom, calls=%fused_computation.clone.1 | custom fusion | bytes 66560 | tf_op jit(solution)/shard_map/while/body/eval_jaxpr/gather | solution.py:112
  210.4 0.7 constant_dynamic-update-slice_fusion.2
  211.1 4.9 %fusion.114 = f32[32,2,128,128]{3,2,1,0:T(8,128)} fusion(bf16[32,2,128,128]{3,2,1,0:T(8,128)(2,1)} %get-tuple-element.198, s32[128]{0:T(128)S(1)} %fusion.113), kind=kOutput, calls=%fused_computation.3.clone.1 | convolution fusion | flops 537952256 | bytes 6291968 | tf_op jit(solution)/shard_map/while/body/eval_jaxpr/kcaj,bj->kcab/dot_general | solution.py:102
  216.0 2.3 convert_element_type.86
  218.3 0.6 copy-done.1
  218.8 1.0 subtract_reduce_fusion.2
  219.8 4.3 %gather_fusion = bf16[128,64,2]{1,2,0:T(2,128)(2,1)S(1)} fusion(bf16[64,2,128,128]{0,1,3,2:T(2,128)(2,1)} %get-tuple-element.200, s32[128]{0:T(128)S(1)} %or_bitcast_fusion.5), kind=kCustom, calls=%fused_computation.1.clone.1 | custom fusion | bytes 66560 | tf_op jit(solution)/shard_map/while/body/eval_jaxpr/gather | solution.py:113
  224.3 4.3 %gather_fusion.1 = bf16[128,64,2]{1,2,0:T(2,128)(2,1)S(1)} fusion(bf16[64,2,128,128]{0,1,3,2:T(2,128)(2,1)} %get-tuple-element.200, s32[128]{0:T(128)S(1)} %get-tuple-element.180), kind=kCustom, calls=%fused_computation.clone.1 | custom fusion | bytes 66560 | tf_op jit(solution)/shard_map/while/body/eval_jaxpr/gather | solution.py:112
  229.8 0.7 constant_dynamic-update-slice_fusion.2
  230.5 4.9 %fusion.114 = f32[32,2,128,128]{3,2,1,0:T(8,128)} fusion(bf16[32,2,128,128]{3,2,1,0:T(8,128)(2,1)} %get-tuple-element.198, s32[128]{0:T(128)S(1)} %fusion.113), kind=kOutput, calls=%fused_computation.3.clone.1 | convolution fusion | flops 537952256 | bytes 6291968 | tf_op jit(solution)/shard_map/while/body/eval_jaxpr/kcaj,bj->kcab/dot_general | solution.py:102
  235.4 2.3 convert_element_type.86
  238.2 1.0 subtract_reduce_fusion.2
  239.2 4.3 %gather_fusion = bf16[128,64,2]{1,2,0:T(2,128)(2,1)S(1)} fusion(bf16[64,2,128,128]{0,1,3,2:T(2,128)(2,1)} %get-tuple-element.200, s32[128]{0:T(128)S(1)} %or_bitcast_fusion.5), kind=kCustom, calls=%fused_computation.1.clone.1 | custom fusion | bytes 66560 | tf_op jit(solution)/shard_map/while/body/eval_jaxpr/gather | solution.py:113
  243.6 4.3 %gather_fusion.1 = bf16[128,64,2]{1,2,0:T(2,128)(2,1)S(1)} fusion(bf16[64,2,128,128]{0,1,3,2:T(2,128)(2,1)} %get-tuple-element.200, s32[128]{0:T(128)S(1)} %get-tuple-element.180), kind=kCustom, calls=%fused_computation.clone.1 | custom fusion | bytes 66560 | tf_op jit(solution)/shard_map/while/body/eval_jaxpr/gather | solution.py:112
  249.2 0.7 constant_dynamic-update-slice_fusion.2
  249.9 4.9 %fusion.114 = f32[32,2,128,128]{3,2,1,0:T(8,128)} fusion(bf16[32,2,128,128]{3,2,1,0:T(8,128)(2,1)} %get-tuple-element.198, s32[128]{0:T(128)S(1)} %fusion.113), kind=kOutput, calls=%fused_computation.3.clone.1 | convolution fusion | flops 537952256 | bytes 6291968 | tf_op jit(solution)/shard_map/while/body/eval_jaxpr/kcaj,bj->kcab/dot_general | solution.py:102
  254.7 2.3 convert_element_type.86
  257.6 1.0 subtract_reduce_fusion.2
  258.5 4.3 %gather_fusion = bf16[128,64,2]{1,2,0:T(2,128)(2,1)S(1)} fusion(bf16[64,2,128,128]{0,1,3,2:T(2,128)(2,1)} %get-tuple-element.200, s32[128]{0:T(128)S(1)} %or_bitcast_fusion.5), kind=kCustom, calls=%fused_computation.1.clone.1 | custom fusion | bytes 66560 | tf_op jit(solution)/shard_map/while/body/eval_jaxpr/gather | solution.py:113
  263.0 4.3 %gather_fusion.1 = bf16[128,64,2]{1,2,0:T(2,128)(2,1)S(1)} fusion(bf16[64,2,128,128]{0,1,3,2:T(2,128)(2,1)} %get-tuple-element.200, s32[128]{0:T(128)S(1)} %get-tuple-element.180), kind=kCustom, calls=%fused_computation.clone.1 | custom fusion | bytes 66560 | tf_op jit(solution)/shard_map/while/body/eval_jaxpr/gather | solution.py:112
  268.6 0.7 constant_dynamic-update-slice_fusion.2
  269.2 1.1 copy.33
  270.4 44.3 %all_to_all.23 = f32[16,2,4,128,8]{3,4,2,1,0:T(8,128)S(1)} all-to-all(f32[16,2,4,128,8]{3,4,2,1,0:T(8,128)S(1)} %copy.33), channel_id=1, replica_groups=mesh['blk'=32,'group'=16] {'group'}, dimensions={0} | all-to-all | bytes 1048576 | tf_op jit(solution)/shard_map/all_to_all | solution.py:29
  315.0 1.2 reshape.322
  316.1 7.4 %all-to-all-start.1 = ((f32[32,1,256]{2,1,0:T(1,128)}), f32[32,1,256]{2,1,0:T(1,128)S(1)}, u32[]{:S(2)}, u32[]{:S(2)}) async-start(f32[32,1,256]{2,1,0:T(1,128)} %reshape.322), calls=%async_computation.1 | async-start | bytes 65536 | tf_op jit(solution)/shard_map/all_to_all | solution.py:142
  323.5 9.1 %all-to-all-done.1 = f32[32,1,256]{2,1,0:T(1,128)S(1)} async-done(((f32[32,1,256]{2,1,0:T(1,128)}), f32[32,1,256]{2,1,0:T(1,128)S(1)}, u32[]{:S(2)}, u32[]{:S(2)}) %all-to-all-start.1) | async-done | bytes 32800 | tf_op jit(solution)/shard_map/all_to_all | solution.py:142
  333.2 0.7 reduce.11
  333.9 0.7 reshape.323
  335.4 4.8 %gather_fusion.2 = f32[512,2,8]{2,1,0:T(2,128)} fusion(f32[2,128,4,8]{3,0,2,1:T(2,128)S(1)} %copy.38, s32[512]{0:T(512)S(1)} %fusion.69), kind=kCustom, calls=%fused_computation.2 | custom fusion | bytes 69632 | tf_op jit(solution)/shard_map/gather | solution.py:144
  340.2 1.2 copy.42
  341.4 0.6 copy.40
  (90 shorter events, 10.4 us)
Async XLA Ops:
  6.5 5.9 %copy-start = (bf16[1,1152,1152]{2,1,0:T(8,128)(2,1)S(1)}, bf16[1,1152,1152]{2,1,0:T(8,128)(2,1)}, u32[]{:S(2)}) copy-start(bf16[1,1152,1152]{2,1,0:T(8,128)(2,1)} %param.9) | copy-start | bytes 7962628
  6.5 161.6 %all-gather.2.cloned.1.call-start = ((), (), s32[]{:S(2)}) async-start(), calls=%async_computation.2 | async-start | bytes 6488064 | tf_op jit(solution)/shard_map/all_gather | solution.py:18
  196.6 2.8 copy-start.1
  216.0 2.8 copy-start.1
  235.4 2.8 copy-start.1
  254.7 2.8 copy-start.1
  269.2 54.3 %copy-start.2 = (s32[4,128]{1,0:T(4,128)S(1)}, s32[4,128]{1,0:T(4,128)}, u32[]{:S(2)}) copy-start(s32[4,128]{1,0:T(4,128)} %param.15) | copy-start | bytes 6148
  316.1 16.5 %all-to-all-start.1 = ((f32[32,1,256]{2,1,0:T(1,128)}), f32[32,1,256]{2,1,0:T(1,128)S(1)}, u32[]{:S(2)}, u32[]{:S(2)}) async-start(f32[32,1,256]{2,1,0:T(1,128)} %reshape.322), calls=%async_computation.1 | async-start | bytes 65536 | tf_op jit(solution)/shard_map/all_to_all | solution.py:142
Sparse Core Ops, SparseCore 0:
  16.4 151.6 all-gather.1
where the time goes:
time: 350 us; the launch traced here: 349 us
  waiting for transfers between devices  160 us (46%)
  local copies, waits for them, and re-layouts  75.6 us (22%)
  blocking collectives  44.3 us (13%)
  matrix products  25.3 us (7%)
  other arithmetic  22.1 us (6%)
  between operations  13.6 us (4%)
  starting transfers between devices  7.36 us (2%)
    all_gather x1, waiting for transfers between devices, sent_together(): out = lax.all_gather(both, axis, axis=dim, tiled=True)  151 us
    all_to_all x1, blocking collectives, sent_and_summed(): lax.all_to_all(in_blocks(value, dim, devices), axis, 0, 0, tiled=True)  44.3 us
    dot_general x4, matrix products, direct_terms(): jnp.einsum('kcaj,bj->kcab', halfway, selector, preferred_element_type=jnp...  19.5 us
    gather x4, local copies, waits for them, and re-layouts, copy_exchange(): lead_values = spin_pieces[:, :, column_ids, perm_row]  17.1 us
    gather x4, local copies, waits for them, and re-layouts, copy_exchange(): trail_values = spin_pieces[:, :, perm_row, column_ids]  17 us
    while x1, local copies, waits for them, and re-layouts, body(): transfer = jnp.swapaxes(lax.map(one_slice, owned_perms), 0, 1)  14.4 us
    all_to_all x1, waiting for transfers between devices, body(): lax.all_to_all(shares, 'blk', split_axis=2, concat_axis=1, tiled=True)  9.13 us
    convert_element_type x4, other arithmetic, direct_terms(): local_copy = sums_piece.astype(jnp.float32)  9.01 us
  transfers between devices with their start and end apart: 2, of which 2 were waited for; matrix products, arithmetic and copies ran while one was open for 0% of the time, Pallas kernels for 0%

commit v1 on v0

v1 whole, which is shorter than its diff:
```python
import functools
import math

import jax
import jax.numpy as jnp
from jax import lax
from jax.experimental import pallas as pl
from jax.experimental.pallas import tpu as pltpu
from jax.sharding import Mesh, PartitionSpec as P

LX = 4
NK = 16
NW = 8
W = 128
NV = 1152
NT = 1024
BROWS = 8
NEAR = 8
VMEM = pl.BlockSpec(memory_space=pltpu.VMEM)
SMEM = pl.BlockSpec(memory_space=pltpu.SMEM)
BF16 = jnp.bfloat16
F32 = jnp.float32


def green_kernel(m_ref, site_ref, time_ref, spin_ref, free_ref, out_ref, rows_ref):
    freq = lax.broadcasted_iota(jnp.int32, (NW, NV), 0)
    times = jnp.broadcast_to(time_ref[...], (NW, NV))
    sites = jnp.broadcast_to(site_ref[...], (NW, NV))
    spins = jnp.broadcast_to(spin_ref[...], (NW, NV))
    winding = ((2 * freq + 1) * times) & (2 * NT - 1)
    angles = winding.astype(F32) * (math.pi / NT)
    cosine, sine = jnp.cos(angles), jnp.sin(angles)
    rx, ry = sites & (LX - 1), sites >> 2
    up = (spins == 0).astype(F32)
    down = (spins == 1).astype(F32)
    blocks = [[], [], [], []]
    for k in range(NK):
        turns = ((k % LX) * rx + (k // LX) * ry) & 3
        odd = (turns & 1) == 1
        sign_c = jnp.where(((turns + 1) & 2) == 0, 1.0, -1.0)
        sign_s = jnp.where((turns & 2) == 0, 1.0, -1.0)
        ck = jnp.where(odd, sine, cosine) * sign_c
        sk = jnp.where(odd, cosine, sine) * sign_s
        for block, value in zip(blocks, (ck * up, sk * up, ck * down, sk * down)):
            block.append(value)
    for index, block in enumerate(blocks):
        rows_ref[index * W : (index + 1) * W, :] = jnp.concatenate(block, 0).astype(BF16)
    norm_factor = 1.0 / math.sqrt(NV)
    eye = lax.broadcasted_iota(jnp.int32, (W, W), 0) == lax.broadcasted_iota(jnp.int32, (W, W), 1)
    fr, fi = free_ref[0:1, :], free_ref[1:2, :]
    col_r = jnp.sum(jnp.where(eye, fr, 0.0), axis=1, keepdims=True)
    col_i = jnp.sum(jnp.where(eye, fi, 0.0), axis=1, keepdims=True)
    for s in range(2):
        rows = rows_ref[2 * W * s : 2 * W * (s + 1), :]
        projected = jnp.dot(rows, m_ref[0], preferred_element_type=F32).astype(BF16)
        pairs = lax.dot_general(
            projected, rows, (((1,), (1,)), ((), ())), preferred_element_type=F32
        )
        kr = pairs[:W, :W] + pairs[W:, W:]
        ki = pairs[W:, :W] - pairs[:W, W:]
        hr = col_r * kr - col_i * ki
        hi = col_r * ki + col_i * kr
        out_ref[2 * s] = (-(hr * fr - hi * fi) * norm_factor).astype(BF16)
        out_ref[2 * s + 1] = (-(hr * fi + hi * fr) * norm_factor).astype(BF16)


def pair_kernel(
    near_ref, own_ref, other_ref, plus_ref, out_ref,
    both_ref, pick_ref, lead_ref, trail_ref, col_ref, sums_ref, flat_ref,
):
    def plane(w, s, part):
        ref = own_ref if w < 4 else other_ref
        return ref[(w % 4) * 4 + 2 * s + part]

    near = near_ref[0]
    plus = plus_ref[...]
    plus_t = plus.astype(F32).T.astype(jnp.int32)
    lane = lax.broadcasted_iota(jnp.int32, (W, W), 1)
    slot = lax.broadcasted_iota(jnp.int32, (16, W), 0)
    point = lax.broadcasted_iota(jnp.int32, (16, W), 1)
    owned = (slot // 8) * 64 + near * 8 + slot % 8
    chosen = (point == owned).astype(BF16)
    plus_own = jnp.dot(chosen, plus_t.astype(F32).astype(BF16), preferred_element_type=F32)
    plus_own_i = plus_own.astype(jnp.int32)
    plus_col = plus_own.T.astype(jnp.int32)
    for b in range(16):
        hot = (plus_col[:, b : b + 1] == lane).astype(F32).astype(BF16)
        pick_ref[b * W : (b + 1) * W, 0:W] = hot
        pick_ref[b * W : (b + 1) * W, W : 2 * W] = hot
    for w in range(NEAR):
        for part in range(2):
            total = None
            for s in range(2):
                value = plane(w, s, part)
                both_ref[w, s * W : (s + 1) * W, part * W : (part + 1) * W] = value
                k = (w * 2 + s) * 2 + part
                lead_ref[k] = jnp.take_along_axis(value.astype(F32), plus_t, axis=1)
                columns = lax.dot_general(
                    chosen, value, (((1,), (1,)), ((), ())), preferred_element_type=F32
                )
                trail_ref[k] = jnp.take_along_axis(columns, plus_own_i, axis=1)
                total = columns if total is None else total + columns
            col_ref[w * 2 + part] = total

    def some(step, carry):
        start = pl.multiple_of(step * 4 * W, 4 * W)
        picks = pick_ref[pl.ds(start, 4 * W), :]
        for w in range(NEAR):
            moved = jnp.dot(picks, both_ref[w], preferred_element_type=F32)
            for j in range(4):
                row_r = col_ref[2 * w, pl.ds(step * 4 + j, 1), :]
                row_i = col_ref[2 * w + 1, pl.ds(step * 4 + j, 1), :]
                yr = jnp.take_along_axis(moved[j * W : (j + 1) * W, :W], plus, axis=1)
                yi = jnp.take_along_axis(moved[j * W : (j + 1) * W, W:], plus, axis=1)
                re = row_r * yr - row_i * yi
                im = row_r * yi + row_i * yr
                if w == 0:
                    sums_ref[2 * j] = re
                    sums_ref[2 * j + 1] = im
                else:
                    sums_ref[2 * j] += re
                    sums_ref[2 * j + 1] += im
        for j in range(4):
            b = step * 4 + j
            er = sums_ref[2 * j].T
            ei = sums_ref[2 * j + 1].T
            for k in range(2 * NEAR):
                lr, li = lead_ref[2 * k], lead_ref[2 * k + 1]
                tr = trail_ref[2 * k, pl.ds(b, 1), :]
                ti = trail_ref[2 * k + 1, pl.ds(b, 1), :]
                er = er - (lr * tr - li * ti)
                ei = ei - (lr * ti + li * tr)
            sums_ref[2 * j] = er
            sums_ref[2 * j + 1] = ei
            for part in range(2):
                for a4 in range(4):
                    piece = sums_ref[2 * j + part, pl.ds(a4, 32, stride=4), :]
                    first = (b // 8) * 64 + (part * 4 + a4) * 8 + b % 8
                    flat_ref[pl.ds(first, 32, stride=128), :] = piece
        return carry

    lax.fori_loop(0, 4, some, 0)
    out_ref[...] = flat_ref[...].astype(BF16)


def last_kernel(parts_ref, cross_ref, out_ref):
    def add(step, total):
        for j in range(8):
            total = total + parts_ref[step * 8 + j].astype(F32)
        return total

    total = lax.fori_loop(0, 8, add, jnp.zeros((64, W), F32))
    for part in range(2):
        for a4 in range(4):
            first = (part * 4 + a4) * 8
            index = jnp.broadcast_to(cross_ref[a4 : a4 + 1, :], (8, W))
            out_ref[part, a4] = jnp.take_along_axis(total[first : first + 8], index, axis=1)


def body(vertex_matrix, vertex_site, vertex_time, vertex_spin, free_green, plus_table, cross_table):
    limit = pltpu.CompilerParams(vmem_limit_bytes=48 << 20)
    green = pl.pallas_call(
        green_kernel,
        out_shape=jax.ShapeDtypeStruct((4, W, W), BF16),
        in_specs=[VMEM] * 5,
        out_specs=VMEM,
        scratch_shapes=[pltpu.VMEM((4 * W, NV), BF16)],
        compiler_params=limit,
        name="green",
    )(vertex_matrix, vertex_site, vertex_time, vertex_spin, free_green)
    own = lax.all_gather(green, "x", axis=0, tiled=True)
    other = lax.ppermute(own, "core", [(0, 1), (1, 0)])
    near = (lax.axis_index("x") * 2 + lax.axis_index("core")).reshape(1)
    partial = pl.pallas_call(
        pair_kernel,
        out_shape=jax.ShapeDtypeStruct((64 * 64, W), BF16),
        in_specs=[SMEM] + [VMEM] * 3,
        out_specs=VMEM,
        scratch_shapes=[
            pltpu.VMEM((NEAR, 2 * W, 2 * W), BF16),
            pltpu.VMEM((16 * W, 2 * W), BF16),
            pltpu.VMEM((4 * NEAR, W, W), F32),
            pltpu.VMEM((4 * NEAR, 16, W), F32),
            pltpu.VMEM((2 * NEAR, 16, W), F32),
            pltpu.VMEM((8, W, W), F32),
            pltpu.VMEM((64 * 64, W), F32),
        ],
        compiler_params=limit,
        name="pairs",
    )(near, own, other, plus_table)
    parts = lax.all_to_all(
        partial.reshape(64, 64, W), ("y", "z_lo", "z_hi"), 0, 0, tiled=True
    )
    crossed = pl.pallas_call(
        last_kernel,
        out_shape=jax.ShapeDtypeStruct((2, 4, BROWS, W), F32),
        in_specs=[VMEM] * 2,
        out_specs=VMEM,
        name="last",
    )(parts, cross_table)
    return jnp.swapaxes(crossed, 2, 3)


def solution(mesh):
    names = ("y", "z_lo", "z_hi", "x", "core")
    fine = Mesh(mesh.devices.reshape(8, 4, 2, 4, 2), names)
    rows = P(names)
    in_specs = (P(names, None, None), rows, rows, rows, P(), P(), P(("y", "z_lo"), None))
    out_specs = P(None, ("y", "z_lo"), None, ("z_hi", "x", "core"))
    return jax.shard_map(body, mesh=fine, in_specs=in_specs, out_specs=out_specs, check_vma=False)
```

time: 350 us -> 99 us (0.28)
  the two profiles are of different devices: /device:TPU:1 before, /device:TPU:2 now
where the time goes in v1:
time: 99 us; the launch traced here: 98.7 us
  blocking collectives  61.9 us (63%)
  Pallas kernels  28.5 us (29%)
  local copies, waits for them, and re-layouts  4.49 us (5%)
  starting transfers between devices  1.91 us (2%)
  waiting for transfers between devices  1.87 us (2%)
    all_to_all x1, blocking collectives, body(): lax.all_to_all(partial.reshape(64, 64, W), ('y', 'z_lo', 'z_hi'), 0, 0, t...  46.5 us
    pallas_call x1, Pallas kernels, body(): pl.pallas_call(pair_kernel, out_shape=jax.ShapeDtypeStruct((64 * 64, W),...  23.7 us
    all_gather x1, blocking collectives, body(): own = lax.all_gather(green, 'x', axis=0, tiled=True)  15.4 us
    unnamed x12, local copies, waits for them, and re-layouts  4.49 us
    pallas_call x1, Pallas kernels, body(): pl.pallas_call(green_kernel, out_shape=jax.ShapeDtypeStruct((4, W, W), BF...  2.75 us
    pallas_call x1, Pallas kernels, body(): pl.pallas_call(last_kernel, out_shape=jax.ShapeDtypeStruct((2, 4, BROWS,...  2.08 us
  transfers between devices with their start and end apart: 1, of which 1 were waited for; matrix products, arithmetic and copies ran while one was open for 0% of the time, Pallas kernels for 0%

profile of v1, /device:TPU:2, one launch (start us, length us, event | category | flops | bytes accessed | tf_op | source)
XLA Modules:
  0.0 98.7 jit_solution(13358943329554330169)
XLA Ops:
  0.0 0.0 copy-start
  0.0 1.7 %copy-done = bf16[1,1152,1152]{2,1,0:T(8,128)(2,1)S(1)} copy-done((bf16[1,1152,1152]{2,1,0:T(8,128)(2,1)S(1)}, bf16[1,1152,1152]{2,1,0:T(8,128)(2,1)}, u32[]{:S(2)}) %copy-start) | copy-done | bytes 2654232
  1.8 0.0 copy-start.2
  1.8 0.7 copy-done.2
  2.4 0.0 copy-start.3
  2.4 0.7 copy-done.3
  3.1 0.0 copy-start.4
  3.1 0.7 copy-done.4
  3.8 0.0 copy-start.5
  3.8 0.7 copy-done.5
  4.5 0.0 copy-start.1
  4.5 2.7 %green.1 = bf16[4,128,128]{2,1,0:T(8,128)(2,1)S(1)} custom-call(bf16[1,1152,1152]{2,1,0:T(8,128)(2,1)S(1)} %copy-done, s32[1,1152]{1,0:T(1,128)S(1)} %copy-done.2, s32[1,1152]{1,0:T(1,128)S(1)} %copy-done.3, s32[1,1152]{1,0:T(1,128)S(1)} %copy-done.4, f32[2,128]{1,0:T(2,128)S(1)} %copy-done.5), custom_call_target="tpu_custom_call" | custom-call | tf_op jit(solution)/shard_map/green/pallas_call | solution.py:162
  7.3 15.4 %all_gather.3.own_ref = bf16[16,128,128]{2,1,0:T(8,128)(2,1)S(1)} all-gather(bf16[4,128,128]{2,1,0:T(8,128)(2,1)S(1)} %green.1), channel_id=1, replica_groups=mesh['y'=8,'z_lo'=4,'z_hi'=2,'x'=4,'core'=2] {'x'}, dimensions={0}, use_global_device_ids=true | all-gather | bytes 655360 | tf_op jit(solution)/shard_map/all_gather | solution.py:171
  22.7 1.9 %collective-permute-start = (bf16[16,128,128]{2,1,0:T(8,128)(2,1)S(1)}, bf16[16,128,128]{2,1,0:T(8,128)(2,1)S(1)}, u32[]{:S(2)}, u32[]{:S(2)}) collective-permute-start(bf16[16,128,128]{2,1,0:T(8,128)(2,1)S(1)} %all_gather.3.own_ref), channel_id=1, source_target_pairs={{0,1},{1,0},{2,3},{3,2},{4,5},{5,4},{6,7},{7,6},{8,9},{9,8},{10,11... | collective-permute-start | bytes 1572872 | tf_op jit(solution)/shard_map/ppermute | solution.py:172
  24.6 1.9 %collective-permute-done.other_ref = bf16[16,128,128]{2,1,0:T(8,128)(2,1)S(1)} collective-permute-done((bf16[16,128,128]{2,1,0:T(8,128)(2,1)S(1)}, bf16[16,128,128]{2,1,0:T(8,128)(2,1)S(1)}, u32[]{:S(2)}, u32[]{:S(2)}) %collective-permute-start) | collective-permute-done | bytes 524320 | tf_op jit(solution)/shard_map/ppermute | solution.py:172
  26.5 0.0 copy-done.1
  26.5 23.7 %pairs.1 = bf16[4096,128]{1,0:T(8,128)(2,1)S(1)} custom-call(s32[1]{0:T(128)} %bitcast.near_ref, bf16[16,128,128]{2,1,0:T(8,128)(2,1)S(1)} %all_gather.3.own_ref, bf16[16,128,128]{2,1,0:T(8,128)(2,1)S(1)} %collective-permute-done.other_ref, s32[128,128]{1,0:T(8,128)S(1)} %copy-done.1), custom_call_target="tpu_custom_call" | custom-call | tf_op jit(solution)/shard_map/pairs/pallas_call | solution.py:174
  50.2 46.5 %all_to_all.5.parts_ref = bf16[64,64,128]{2,1,0:T(8,128)(2,1)} all-to-all(bf16[64,64,128]{2,1,0:T(8,128)(2,1)S(1)} %bitcast.3), channel_id=1, replica_groups=mesh['y'=8,'z_lo'=4,'z_hi'=2,'x'=4,'core'=2] {'y','z_lo','z_hi'}, dimensions={0} | all-to-all | bytes 2097152 | tf_op jit(solution)/shard_map/all_to_all | solution.py:191
  96.6 2.1 %last.1 = f32[2,4,8,128]{3,2,1,0:T(8,128)} custom-call(bf16[64,64,128]{2,1,0:T(8,128)(2,1)} %all_to_all.5.parts_ref, s32[4,128]{1,0:T(4,128)} %cross_ref.1), custom_call_target="tpu_custom_call" | custom-call | tf_op jit(solution)/shard_map/last/pallas_call | solution.py:194
Async XLA Ops:
  0.0 1.7 %copy-start = (bf16[1,1152,1152]{2,1,0:T(8,128)(2,1)S(1)}, bf16[1,1152,1152]{2,1,0:T(8,128)(2,1)}, u32[]{:S(2)}) copy-start(bf16[1,1152,1152]{2,1,0:T(8,128)(2,1)} %m_ref.1) | copy-start | bytes 7962628
  1.8 0.7 copy-start.2
  2.4 0.7 copy-start.3
  3.1 0.7 copy-start.4
  3.8 0.7 copy-start.5
  4.5 22.0 %copy-start.1 = (s32[128,128]{1,0:T(8,128)S(1)}, s32[128,128]{1,0:T(8,128)}, u32[]{:S(2)}) copy-start(s32[128,128]{1,0:T(8,128)} %plus_ref.1) | copy-start | bytes 196612
  22.7 3.8 %collective-permute-start = (bf16[16,128,128]{2,1,0:T(8,128)(2,1)S(1)}, bf16[16,128,128]{2,1,0:T(8,128)(2,1)S(1)}, u32[]{:S(2)}, u32[]{:S(2)}) collective-permute-start(bf16[16,128,128]{2,1,0:T(8,128)(2,1)S(1)} %all_gather.3.own_ref), channel_id=1, source_target_pairs={{0,1},{1,0},{2,3},{3,2},{4,5},{5,4},{6,7},{7,6},{8,9},{9,8},{10,11... | collective-permute-start | bytes 1572872 | tf_op jit(solution)/shard_map/ppermute | solution.py:172

commit v2 on v1

v2 whole, which is shorter than its diff:
```python
import functools
import math

import jax
import jax.numpy as jnp
from jax import lax
from jax.experimental import pallas as pl
from jax.experimental.pallas import tpu as pltpu
from jax.sharding import Mesh, PartitionSpec as P

LX = 4
NK = 16
NW = 8
W = 128
NV = 1152
NT = 1024
BROWS = 8
NEAR = 8
PIECE = 384
PITCH = W + 1
STEP = 4 * NEAR + 1
HBM = pl.BlockSpec(memory_space=pltpu.HBM)
VMEM = pl.BlockSpec(memory_space=pltpu.VMEM)
SMEM = pl.BlockSpec(memory_space=pltpu.SMEM)
BF16 = jnp.bfloat16
F32 = jnp.float32


def green_kernel(
    m_hbm, site_hbm, time_hbm, spin_hbm, free_hbm, out_ref,
    m_ref, site_ref, time_ref, spin_ref, free_ref, rows_ref, sems,
):
    small = [
        pltpu.make_async_copy(src, dst, sems.at[i])
        for i, (src, dst) in enumerate(
            ((site_hbm, site_ref), (time_hbm, time_ref), (spin_hbm, spin_ref), (free_hbm, free_ref))
        )
    ]
    large = [
        pltpu.make_async_copy(
            m_hbm.at[0, :, c * PIECE : (c + 1) * PIECE],
            m_ref.at[:, c * PIECE : (c + 1) * PIECE],
            sems.at[4 + c],
        )
        for c in range(NV // PIECE)
    ]
    for copy in small + large:
        copy.start()
    for copy in small:
        copy.wait()
    freq = lax.broadcasted_iota(jnp.int32, (NW, NV), 0)
    times = jnp.broadcast_to(time_ref[...], (NW, NV))
    sites = jnp.broadcast_to(site_ref[...], (NW, NV))
    spins = jnp.broadcast_to(spin_ref[...], (NW, NV))
    winding = ((2 * freq + 1) * times) & (2 * NT - 1)
    angles = winding.astype(F32) * (math.pi / NT)
    cosine, sine = jnp.cos(angles), jnp.sin(angles)
    rx, ry = sites & (LX - 1), sites >> 2
    up = (spins == 0).astype(F32)
    down = (spins == 1).astype(F32)
    for pair in range(NK // 2):
        blocks = [[], [], [], []]
        for k in (2 * pair, 2 * pair + 1):
            turns = ((k % LX) * rx + (k // LX) * ry) & 3
            odd = (turns & 1) == 1
            sign_c = jnp.where(((turns + 1) & 2) == 0, 1.0, -1.0)
            sign_s = jnp.where((turns & 2) == 0, 1.0, -1.0)
            ck = jnp.where(odd, sine, cosine) * sign_c
            sk = jnp.where(odd, cosine, sine) * sign_s
            for block, value in zip(blocks, (ck * up, sk * up, ck * down, sk * down)):
                block.append(value)
        for index, block in enumerate(blocks):
            first = index * W + pair * 2 * NW
            rows_ref[first : first + 2 * NW, :] = jnp.concatenate(block, 0).astype(BF16)
    norm_factor = 1.0 / math.sqrt(NV)
    eye = lax.broadcasted_iota(jnp.int32, (W, W), 0) == lax.broadcasted_iota(jnp.int32, (W, W), 1)
    fr, fi = free_ref[0:1, :], free_ref[1:2, :]
    col_r = jnp.sum(jnp.where(eye, fr, 0.0), axis=1, keepdims=True)
    col_i = jnp.sum(jnp.where(eye, fi, 0.0), axis=1, keepdims=True)
    pairs = [None, None]
    for c in range(NV // PIECE):
        large[c].wait()
        piece = m_ref[:, c * PIECE : (c + 1) * PIECE]
        for s in range(2):
            mine = slice(2 * W * s, 2 * W * (s + 1))
            projected = jnp.dot(rows_ref[mine, :], piece, preferred_element_type=F32)
            term = lax.dot_general(
                projected.astype(BF16),
                rows_ref[mine, c * PIECE : (c + 1) * PIECE],
                (((1,), (1,)), ((), ())),
                preferred_element_type=F32,
            )
            pairs[s] = term if c == 0 else pairs[s] + term
    for s in range(2):
        kr = pairs[s][:W, :W] + pairs[s][W:, W:]
        ki = pairs[s][W:, :W] - pairs[s][:W, W:]
        hr = col_r * kr - col_i * ki
        hi = col_r * ki + col_i * kr
        out_ref[2 * s] = (-(hr * fr - hi * fi) * norm_factor).astype(BF16)
        out_ref[2 * s + 1] = (-(hr * fi + hi * fr) * norm_factor).astype(BF16)


def pair_kernel(
    near_ref, own_ref, other_ref, plus_ref, out_ref,
    both_ref, pick_ref, lead_ref, trail_ref, spread_ref, col_ref, even_ref, odd_ref,
    sums_ref, turn_ref,
):
    def plane(w, s, part):
        ref = own_ref if w < 4 else other_ref
        return ref[(w % 4) * 4 + 2 * s + part]

    near = near_ref[0]
    plus_t = plus_ref[...].astype(F32).T.astype(jnp.int32)
    lane = lax.broadcasted_iota(jnp.int32, (W, W), 1)
    slot = lax.broadcasted_iota(jnp.int32, (16, W), 0)
    point = lax.broadcasted_iota(jnp.int32, (16, W), 1)
    owned = (slot // 8) * 64 + near * 8 + slot % 8
    chosen = (point == owned).astype(BF16)
    plus_own = jnp.dot(chosen, plus_t.astype(F32).astype(BF16), preferred_element_type=F32)
    plus_own_i = plus_own.astype(jnp.int32)
    plus_col = plus_own.T.astype(jnp.int32)
    for b in range(16):
        hot = (plus_col[:, b : b + 1] == lane).astype(F32).astype(BF16)
        pick_ref[b * W : (b + 1) * W, 0:W] = hot
        pick_ref[b * W : (b + 1) * W, W : 2 * W] = hot
    for w in range(NEAR):
        for part in range(2):
            total = None
            for s in range(2):
                value = plane(w, s, part)
                both_ref[w, s * W : (s + 1) * W, part * W : (part + 1) * W] = value
                k = (w * 2 + s) * 2 + part
                lead_ref[k * PITCH : k * PITCH + W, :] = jnp.take_along_axis(
                    value.astype(F32), plus_t, axis=1
                ).T
                columns = lax.dot_general(
                    chosen, value, (((1,), (1,)), ((), ())), preferred_element_type=F32
                )
                trail_ref[pl.ds(k, 16, stride=STEP), :] = jnp.take_along_axis(
                    columns, plus_own_i, axis=1
                )
                total = columns if total is None else total + columns
            col_ref[w * 2 + part] = total

    planes = 4 * NEAR
    from_k = lax.broadcasted_iota(jnp.int32, (planes, 16 * planes), 0)
    to_lane = lax.broadcasted_iota(jnp.int32, (planes, 16 * planes), 1)
    to_k = to_lane & (planes - 1)
    real = to_lane < 8 * planes
    repeat = jnp.where(
        real,
        jnp.where(from_k == to_k, jnp.where((to_k & 1) == 1, 1.0, -1.0), 0.0),
        jnp.where(from_k == (to_k ^ 1), -1.0, 0.0),
    ).astype(BF16)
    on = (
        (lax.broadcasted_iota(jnp.int32, (8, 16 * planes), 1) // planes) % 8
        == lax.broadcasted_iota(jnp.int32, (8, 16 * planes), 0)
    ).astype(F32)
    for b in range(16):
        turned = trail_ref[b * STEP : b * STEP + planes, :].T.astype(BF16)
        spread_ref[b * W : (b + 1) * W, :] = jnp.dot(
            turned, repeat, preferred_element_type=F32
        ) * jnp.tile(on, (16, 1))
    def exchange(t, carry):
        left = jnp.concatenate(
            [
                spread_ref[
                    pl.ds(pl.multiple_of(b * W + t * 8, 8), 8),
                    part * 8 * planes : (part + 1) * 8 * planes,
                ]
                for part in range(2)
                for b in range(16)
            ],
            0,
        ).astype(BF16)
        right = jnp.concatenate(
            [lead_ref[pl.ds(t * 8 + j, planes, stride=PITCH), :] for j in range(8)], 0
        ).astype(BF16)
        term = jnp.dot(left, right, preferred_element_type=F32)
        for part in range(2):
            for b in range(16):
                first = (part * 16 + b) * 8
                sums_ref[2 * b + part, pl.ds(pl.multiple_of(t * 8, 8), 8), :] = term[first : first + 8]
        return carry

    lax.fori_loop(0, 16, exchange, 0)

    def fetch(group, w, dst):
        picks = pick_ref[group * 4 * W : (group + 1) * 4 * W, :]
        dst[w] = jnp.dot(picks, both_ref[w], preferred_element_type=F32)

    buffers = (even_ref, odd_ref)
    for w in range(NEAR):
        fetch(0, w, even_ref)
    for group in range(4):
        now, later = buffers[group % 2], buffers[(group + 1) % 2]

        def direct(step, carry):
            for half in range(4):
                if group < 3 and half % 2 == 0:
                    fetch(group + 1, step * 2 + half // 2, later)
                start = pl.multiple_of(step * 32 + half * 8, 8)
                rows = pl.ds(start, 8)
                index = plus_ref[rows, :]
                for j in range(4):
                    b = group * 4 + j
                    mine = pl.ds(pl.multiple_of(j * W + start, 8), 8)
                    re, im = sums_ref[2 * b, rows, :], sums_ref[2 * b + 1, rows, :]
                    for v in range(NEAR):
                        row_r = col_ref[2 * v, pl.ds(b, 8, stride=0), :]
                        row_i = col_ref[2 * v + 1, pl.ds(b, 8, stride=0), :]
                        yr = jnp.take_along_axis(now[v, mine, 0:W], index, axis=1)
                        yi = jnp.take_along_axis(now[v, mine, W : 2 * W], index, axis=1)
                        re = re + (row_r * yr - row_i * yi)
                        im = im + (row_r * yi + row_i * yr)
                    sums_ref[2 * b, rows, :] = re
                    sums_ref[2 * b + 1, rows, :] = im
            return carry

        lax.fori_loop(0, W // 32, direct, 0)

    def turn(step, carry):
        for j in range(4):
            b = step * 4 + j
            for part in range(2):
                turn_ref[pl.ds((part * 16 + b) * PITCH, W), :] = sums_ref[2 * b + part].T
        return carry

    lax.fori_loop(0, 4, turn, 0)

    def place(step, carry):
        for near_i, high in ((0, 0), (0, 1), (1, 0), (1, 1), (2, 0), (2, 1), (3, 0), (3, 1)):
            i = step * 4 + near_i
            for part in range(2):
                for a4 in (0, 2):
                    tiles = [
                        turn_ref[pl.ds((part * 16 + high * 8) * PITCH + i * 4 + a, 8, stride=PITCH), :]
                        for a in (a4, a4 + 1)
                    ]
                    first = pl.multiple_of((i * 2 + high) * 64 + (part * 4 + a4) * 8, 16)
                    out_ref[pl.ds(first, 16), :] = jnp.concatenate(tiles, 0).astype(BF16)
        return carry

    lax.fori_loop(0, 8, place, 0)


def last_kernel(parts_ref, cross_ref, out_ref):
    def add(step, total):
        for j in range(8):
            total = total + parts_ref[step * 8 + j].astype(F32)
        return total

    total = lax.fori_loop(0, 8, add, jnp.zeros((64, W), F32))
    for part in range(2):
        for a4 in range(4):
            first = (part * 4 + a4) * 8
            index = jnp.broadcast_to(cross_ref[a4 : a4 + 1, :], (8, W))
            out_ref[part, a4] = jnp.take_along_axis(total[first : first + 8], index, axis=1)


def body(vertex_matrix, vertex_site, vertex_time, vertex_spin, free_green, plus_table, cross_table):
    limit = pltpu.CompilerParams(vmem_limit_bytes=48 << 20)
    green = pl.pallas_call(
        green_kernel,
        out_shape=jax.ShapeDtypeStruct((4, W, W), BF16),
        in_specs=[HBM] * 5,
        out_specs=VMEM,
        scratch_shapes=[
            pltpu.VMEM((NV, NV), BF16),
            pltpu.VMEM((1, NV), jnp.int32),
            pltpu.VMEM((1, NV), jnp.int32),
            pltpu.VMEM((1, NV), jnp.int32),
            pltpu.VMEM((2, W), F32),
            pltpu.VMEM((4 * W, NV), BF16),
            pltpu.SemaphoreType.DMA((4 + NV // PIECE,)),
        ],
        compiler_params=limit,
        name="green",
    )(vertex_matrix, vertex_site, vertex_time, vertex_spin, free_green)
    own = lax.all_gather(green, "x", axis=0, tiled=True)
    other = lax.ppermute(own, "core", [(0, 1), (1, 0)])
    near = (lax.axis_index("x") * 2 + lax.axis_index("core")).reshape(1)
    partial = pl.pallas_call(
        pair_kernel,
        out_shape=jax.ShapeDtypeStruct((64 * 64, W), BF16),
        in_specs=[SMEM] + [VMEM] * 3,
        out_specs=VMEM,
        scratch_shapes=[
            pltpu.VMEM((NEAR, 2 * W, 2 * W), BF16),
            pltpu.VMEM((16 * W, 2 * W), BF16),
            pltpu.VMEM((4 * NEAR * PITCH, W), F32),
            pltpu.VMEM((16 * STEP, W), F32),
            pltpu.VMEM((16 * W, 16 * 4 * NEAR), F32),
            pltpu.VMEM((2 * NEAR, 16, W), F32),
            pltpu.VMEM((NEAR, 4 * W, 2 * W), F32),
            pltpu.VMEM((NEAR, 4 * W, 2 * W), F32),
            pltpu.VMEM((32, W, W), F32),
            pltpu.VMEM((32 * PITCH, W), F32),
        ],
        compiler_params=limit,
        name="pairs",
    )(near, own, other, plus_table)
    parts = lax.all_to_all(
        partial.reshape(64, 64, W), ("y", "z_lo", "z_hi"), 0, 0, tiled=True
    )
    crossed = pl.pallas_call(
        last_kernel,
        out_shape=jax.ShapeDtypeStruct((2, 4, BROWS, W), F32),
        in_specs=[VMEM] * 2,
        out_specs=VMEM,
        name="last",
    )(parts, cross_table)
    return jnp.swapaxes(crossed, 2, 3)


def solution(mesh):
    names = ("y", "z_lo", "z_hi", "x", "core")
    fine = Mesh(mesh.devices.reshape(8, 4, 2, 4, 2), names)
    rows = P(names)
    in_specs = (P(names, None, None), rows, rows, rows, P(), P(), P(("y", "z_lo"), None))
    out_specs = P(None, ("y", "z_lo"), None, ("z_hi", "x", "core"))
    return jax.shard_map(body, mesh=fine, in_specs=in_specs, out_specs=out_specs, check_vma=False)
```

time: 99 us -> 90 us (0.909)
  Pallas kernels: 28.5 us -> 19.5 us
    pallas_call x1, Pallas kernels: 23.7 us -> 13.2 us  [body(): pl.pallas_call(pair_kernel, out_shape=jax.ShapeDtypeStruct((64 * 64, W),...]
    pallas_call x1, Pallas kernels: 2.75 us -> 4.24 us  [body(): pl.pallas_call(green_kernel, out_shape=jax.ShapeDtypeStruct((4, W, W), BF...]
where the time goes in v2:
time: 90 us; the launch traced here: 89.7 us
  blocking collectives  61.9 us (69%)
  Pallas kernels  19.5 us (22%)
  local copies, waits for them, and re-layouts  4.49 us (5%)
  starting transfers between devices  1.91 us (2%)
  waiting for transfers between devices  1.87 us (2%)
    all_to_all x1, blocking collectives, body(): lax.all_to_all(partial.reshape(64, 64, W), ('y', 'z_lo', 'z_hi'), 0, 0, t...  46.4 us
    all_gather x1, blocking collectives, body(): own = lax.all_gather(green, 'x', axis=0, tiled=True)  15.4 us
    pallas_call x1, Pallas kernels, body(): pl.pallas_call(pair_kernel, out_shape=jax.ShapeDtypeStruct((64 * 64, W),...  13.2 us
    unnamed x12, local copies, waits for them, and re-layouts  4.49 us
    pallas_call x1, Pallas kernels, body(): pl.pallas_call(green_kernel, out_shape=jax.ShapeDtypeStruct((4, W, W), BF...  4.24 us
    pallas_call x1, Pallas kernels, body(): pl.pallas_call(last_kernel, out_shape=jax.ShapeDtypeStruct((2, 4, BROWS,...  2.08 us
    ppermute x1, starting transfers between devices, body(): other = lax.ppermute(own, 'core', [(0, 1), (1, 0)])  1.91 us
    ppermute x1, waiting for transfers between devices, body(): other = lax.ppermute(own, 'core', [(0, 1), (1, 0)])  1.87 us
  transfers between devices with their start and end apart: 1, of which 1 were waited for; matrix products, arithmetic and copies ran while one was open for 0% of the time, Pallas kernels for 0%

profile of v2, /device:TPU:2, one launch (start us, length us, event | category | flops | bytes accessed | tf_op | source)
XLA Modules:
  0.0 89.7 jit_solution(5541536208207538677)
XLA Ops:
  0.0 0.0 copy-start
  0.0 1.7 %copy-done = bf16[1,1152,1152]{2,1,0:T(8,128)(2,1)S(1)} copy-done((bf16[1,1152,1152]{2,1,0:T(8,128)(2,1)S(1)}, bf16[1,1152,1152]{2,1,0:T(8,128)(2,1)}, u32[]{:S(2)}) %copy-start) | copy-done | bytes 2654232
  1.8 0.0 copy-start.2
  1.8 0.7 copy-done.2
  2.4 0.0 copy-start.3
  2.4 0.7 copy-done.3
  3.1 0.0 copy-start.4
  3.1 0.7 copy-done.4
  3.8 0.0 copy-start.5
  3.8 0.7 copy-done.5
  4.5 0.0 copy-start.1
  4.5 4.2 %green.1 = bf16[4,128,128]{2,1,0:T(8,128)(2,1)S(1)} custom-call(bf16[1,1152,1152]{2,1,0:T(8,128)(2,1)S(1)} %copy-done, s32[1,1152]{1,0:T(1,128)S(1)} %copy-done.2, s32[1,1152]{1,0:T(1,128)S(1)} %copy-done.3, s32[1,1152]{1,0:T(1,128)S(1)} %copy-done.4, f32[2,128]{1,0:T(2,128)S(1)} %copy-done.5), custom_call_target="tpu_custom_call" | custom-call | tf_op jit(solution)/shard_map/green/pallas_call | solution.py:263
  8.7 15.4 %all_gather.3.own_ref = bf16[16,128,128]{2,1,0:T(8,128)(2,1)S(1)} all-gather(bf16[4,128,128]{2,1,0:T(8,128)(2,1)S(1)} %green.1), channel_id=1, replica_groups=mesh['y'=8,'z_lo'=4,'z_hi'=2,'x'=4,'core'=2] {'x'}, dimensions={0}, use_global_device_ids=true | all-gather | bytes 655360 | tf_op jit(solution)/shard_map/all_gather | solution.py:280
  24.2 1.9 %collective-permute-start = (bf16[16,128,128]{2,1,0:T(8,128)(2,1)S(1)}, bf16[16,128,128]{2,1,0:T(8,128)(2,1)S(1)}, u32[]{:S(2)}, u32[]{:S(2)}) collective-permute-start(bf16[16,128,128]{2,1,0:T(8,128)(2,1)S(1)} %all_gather.3.own_ref), channel_id=1, source_target_pairs={{0,1},{1,0},{2,3},{3,2},{4,5},{5,4},{6,7},{7,6},{8,9},{9,8},{10,11... | collective-permute-start | bytes 1572872 | tf_op jit(solution)/shard_map/ppermute | solution.py:281
  26.1 1.9 %collective-permute-done.other_ref = bf16[16,128,128]{2,1,0:T(8,128)(2,1)S(1)} collective-permute-done((bf16[16,128,128]{2,1,0:T(8,128)(2,1)S(1)}, bf16[16,128,128]{2,1,0:T(8,128)(2,1)S(1)}, u32[]{:S(2)}, u32[]{:S(2)}) %collective-permute-start) | collective-permute-done | bytes 524320 | tf_op jit(solution)/shard_map/ppermute | solution.py:281
  28.0 0.0 copy-done.1
  28.0 13.2 %pairs.1 = bf16[4096,128]{1,0:T(8,128)(2,1)S(1)} custom-call(s32[1]{0:T(128)} %bitcast.near_ref, bf16[16,128,128]{2,1,0:T(8,128)(2,1)S(1)} %all_gather.3.own_ref, bf16[16,128,128]{2,1,0:T(8,128)(2,1)S(1)} %collective-permute-done.other_ref, s32[128,128]{1,0:T(8,128)S(1)} %copy-done.1), custom_call_target="tpu_custom_call" | custom-call | tf_op jit(solution)/shard_map/pairs/pallas_call | solution.py:283
  41.2 46.4 %all_to_all.5.parts_ref = bf16[64,64,128]{2,1,0:T(8,128)(2,1)} all-to-all(bf16[64,64,128]{2,1,0:T(8,128)(2,1)S(1)} %bitcast.3), channel_id=1, replica_groups=mesh['y'=8,'z_lo'=4,'z_hi'=2,'x'=4,'core'=2] {'y','z_lo','z_hi'}, dimensions={0} | all-to-all | bytes 2097152 | tf_op jit(solution)/shard_map/all_to_all | solution.py:303
  87.6 2.1 %last.1 = f32[2,4,8,128]{3,2,1,0:T(8,128)} custom-call(bf16[64,64,128]{2,1,0:T(8,128)(2,1)} %all_to_all.5.parts_ref, s32[4,128]{1,0:T(4,128)} %cross_ref.1), custom_call_target="tpu_custom_call" | custom-call | tf_op jit(solution)/shard_map/last/pallas_call | solution.py:306
Async XLA Ops:
  0.0 1.7 %copy-start = (bf16[1,1152,1152]{2,1,0:T(8,128)(2,1)S(1)}, bf16[1,1152,1152]{2,1,0:T(8,128)(2,1)}, u32[]{:S(2)}) copy-start(bf16[1,1152,1152]{2,1,0:T(8,128)(2,1)} %m_hbm.1) | copy-start | bytes 7962628
  1.8 0.7 copy-start.2
  2.4 0.7 copy-start.3
  3.1 0.7 copy-start.4
  3.8 0.7 copy-start.5
  4.5 23.5 %copy-start.1 = (s32[128,128]{1,0:T(8,128)S(1)}, s32[128,128]{1,0:T(8,128)}, u32[]{:S(2)}) copy-start(s32[128,128]{1,0:T(8,128)} %plus_ref.1) | copy-start | bytes 196612
  24.2 3.8 %collective-permute-start = (bf16[16,128,128]{2,1,0:T(8,128)(2,1)S(1)}, bf16[16,128,128]{2,1,0:T(8,128)(2,1)S(1)}, u32[]{:S(2)}, u32[]{:S(2)}) collective-permute-start(bf16[16,128,128]{2,1,0:T(8,128)(2,1)S(1)} %all_gather.3.own_ref), channel_id=1, source_target_pairs={{0,1},{1,0},{2,3},{3,2},{4,5},{5,4},{6,7},{7,6},{8,9},{9,8},{10,11... | collective-permute-start | bytes 1572872 | tf_op jit(solution)/shard_map/ppermute | solution.py:281

commit v3 on v2

--- a/solution.py
+++ b/solution.py
@@ -19,7 +19,7 @@
 PIECE = 384
 PITCH = W + 1
 STEP = 4 * NEAR + 1
-HBM = pl.BlockSpec(memory_space=pltpu.HBM)
+ANY = pl.BlockSpec(memory_space=pl.ANY)
 VMEM = pl.BlockSpec(memory_space=pltpu.VMEM)
 SMEM = pl.BlockSpec(memory_space=pltpu.SMEM)
 BF16 = jnp.bfloat16
@@ -103,7 +103,7 @@
 def pair_kernel(
     near_ref, own_ref, other_ref, plus_ref, out_ref,
     both_ref, pick_ref, lead_ref, trail_ref, spread_ref, col_ref, even_ref, odd_ref,
-    sums_ref, turn_ref,
+    sums_ref, straight_ref, turn_ref,
 ):
     def plane(w, s, part):
         ref = own_ref if w < 4 else other_ref
@@ -123,6 +123,12 @@
         hot = (plus_col[:, b : b + 1] == lane).astype(F32).astype(BF16)
         pick_ref[b * W : (b + 1) * W, 0:W] = hot
         pick_ref[b * W : (b + 1) * W, W : 2 * W] = hot
+    eye = (lax.broadcasted_iota(jnp.int32, (W, W), 0) == lane).astype(F32).astype(BF16)
+
+    def fetch(group, w, dst):
+        picks = pick_ref[group * 4 * W : (group + 1) * 4 * W, :]
+        dst[w] = jnp.dot(picks, both_ref[w], preferred_element_type=F32)
+
     for w in range(NEAR):
         for part in range(2):
             total = None
@@ -130,9 +136,10 @@
                 value = plane(w, s, part)
                 both_ref[w, s * W : (s + 1) * W, part * W : (part + 1) * W] = value
                 k = (w * 2 + s) * 2 + part
-                lead_ref[k * PITCH : k * PITCH + W, :] = jnp.take_along_axis(
-                    value.astype(F32), plus_t, axis=1
-                ).T
+                lead = jnp.take_along_axis(value.astype(F32), plus_t, axis=1).astype(BF16)
+                lead_ref[k * PITCH : k * PITCH + W, :] = lax.dot_general(
+                    eye, lead, (((1,), (1,)), ((), ())), preferred_element_type=F32
+                )
                 columns = lax.dot_general(
                     chosen, value, (((1,), (1,)), ((), ())), preferred_element_type=F32
                 )
@@ -141,6 +148,7 @@
                 )
                 total = columns if total is None else total + columns
             col_ref[w * 2 + part] = total
+        fetch(0, w, even_ref)
 
     planes = 4 * NEAR
     from_k = lax.broadcasted_iota(jnp.int32, (planes, 16 * planes), 0)
@@ -161,7 +169,8 @@
         spread_ref[b * W : (b + 1) * W, :] = jnp.dot(
             turned, repeat, preferred_element_type=F32
         ) * jnp.tile(on, (16, 1))
-    def exchange(t, carry):
+
+    def exchange(t):
         left = jnp.concatenate(
             [
                 spread_ref[
@@ -181,17 +190,8 @@
             for b in range(16):
                 first = (part * 16 + b) * 8
                 sums_ref[2 * b + part, pl.ds(pl.multiple_of(t * 8, 8), 8), :] = term[first : first + 8]
-        return carry
-
-    lax.fori_loop(0, 16, exchange, 0)
-
-    def fetch(group, w, dst):
-        picks = pick_ref[group * 4 * W : (group + 1) * 4 * W, :]
-        dst[w] = jnp.dot(picks, both_ref[w], preferred_element_type=F32)
 
     buffers = (even_ref, odd_ref)
-    for w in range(NEAR):
-        fetch(0, w, even_ref)
     for group in range(4):
         now, later = buffers[group % 2], buffers[(group + 1) % 2]
 
@@ -205,16 +205,19 @@
                 for j in range(4):
                     b = group * 4 + j
                     mine = pl.ds(pl.multiple_of(j * W + start, 8), 8)
-                    re, im = sums_ref[2 * b, rows, :], sums_ref[2 * b + 1, rows, :]
+                    re = im = None
                     for v in range(NEAR):
                         row_r = col_ref[2 * v, pl.ds(b, 8, stride=0), :]
                         row_i = col_ref[2 * v + 1, pl.ds(b, 8, stride=0), :]
                         yr = jnp.take_along_axis(now[v, mine, 0:W], index, axis=1)
                         yi = jnp.take_along_axis(now[v, mine, W : 2 * W], index, axis=1)
-                        re = re + (row_r * yr - row_i * yi)
-                        im = im + (row_r * yi + row_i * yr)
-                    sums_ref[2 * b, rows, :] = re
-                    sums_ref[2 * b + 1, rows, :] = im
+                        add_r, add_i = row_r * yr - row_i * yi, row_r * yi + row_i * yr
+                        re = add_r if v == 0 else re + add_r
+                        im = add_i if v == 0 else im + add_i
+                    straight_ref[2 * b, rows, :] = re
+                    straight_ref[2 * b + 1, rows, :] = im
+                if group == 0:
+                    exchange(step * 4 + half)
             return carry
 
         lax.fori_loop(0, W // 32, direct, 0)
@@ -223,7 +226,7 @@
         for j in range(4):
             b = step * 4 + j
             for part in range(2):
-                turn_ref[pl.ds((part * 16 + b) * PITCH, W), :] = sums_ref[2 * b + part].T
+                turn_ref[pl.ds((part * 16 + b) * PITCH, W), :] = (straight_ref[2 * b + part] + sums_ref[2 * b + part]).T
         return carry
 
     lax.fori_loop(0, 4, turn, 0)
@@ -263,7 +266,7 @@
     green = pl.pallas_call(
         green_kernel,
         out_shape=jax.ShapeDtypeStruct((4, W, W), BF16),
-        in_specs=[HBM] * 5,
+        in_specs=[ANY] * 5,
         out_specs=VMEM,
         scratch_shapes=[
             pltpu.VMEM((NV, NV), BF16),
@@ -274,7 +277,7 @@
             pltpu.VMEM((4 * W, NV), BF16),
             pltpu.SemaphoreType.DMA((4 + NV // PIECE,)),
         ],
-        compiler_params=limit,
+        compiler_params=pltpu.CompilerParams(vmem_limit_bytes=67043328),
         name="green",
     )(vertex_matrix, vertex_site, vertex_time, vertex_spin, free_green)
     own = lax.all_gather(green, "x", axis=0, tiled=True)
@@ -295,6 +298,7 @@
             pltpu.VMEM((NEAR, 4 * W, 2 * W), F32),
             pltpu.VMEM((NEAR, 4 * W, 2 * W), F32),
             pltpu.VMEM((32, W, W), F32),
+            pltpu.VMEM((32, W, W), F32),
             pltpu.VMEM((32 * PITCH, W), F32),
         ],
         compiler_params=limit,

time: 90 us -> 85.1 us (0.946)
  local copies, waits for them, and re-layouts: 4.49 us -> 0.84 us
  Pallas kernels: 19.5 us -> 18 us
    unnamed x12 -> x2, local copies, waits for them, and re-layouts: 4.49 us -> 0.84 us
    pallas_call x1, Pallas kernels: 13.2 us -> 10.7 us  [body(): pl.pallas_call(pair_kernel, out_shape=jax.ShapeDtypeStruct((64 * 64, W),...]
    pallas_call x1, Pallas kernels: 4.24 us -> 5.31 us  [body(): pl.pallas_call(green_kernel, out_shape=jax.ShapeDtypeStruct((4, W, W), BF...]
where the time goes in v3:
time: 85.1 us; the launch traced here: 84.8 us
  blocking collectives  62.1 us (73%)
  Pallas kernels  18 us (21%)
  starting transfers between devices  1.91 us (2%)
  waiting for transfers between devices  1.87 us (2%)
    all_to_all x1, blocking collectives, body(): lax.all_to_all(partial.reshape(64, 64, W), ('y', 'z_lo', 'z_hi'), 0, 0, t...  46.4 us
    all_gather x1, blocking collectives, body(): own = lax.all_gather(green, 'x', axis=0, tiled=True)  15.7 us
    pallas_call x1, Pallas kernels, body(): pl.pallas_call(pair_kernel, out_shape=jax.ShapeDtypeStruct((64 * 64, W),...  10.7 us
    pallas_call x1, Pallas kernels, body(): pl.pallas_call(green_kernel, out_shape=jax.ShapeDtypeStruct((4, W, W), BF...  5.31 us
    pallas_call x1, Pallas kernels, body(): pl.pallas_call(last_kernel, out_shape=jax.ShapeDtypeStruct((2, 4, BROWS,...  2.08 us
    ppermute x1, starting transfers between devices, body(): other = lax.ppermute(own, 'core', [(0, 1), (1, 0)])  1.91 us
    ppermute x1, waiting for transfers between devices, body(): other = lax.ppermute(own, 'core', [(0, 1), (1, 0)])  1.87 us
  transfers between devices with their start and end apart: 1, of which 1 were waited for; matrix products, arithmetic and copies ran while one was open for 0% of the time, Pallas kernels for 0%

profile of v3, /device:TPU:2, one launch (start us, length us, event | category | flops | bytes accessed | tf_op | source)
XLA Modules:
  0.0 84.8 jit_solution(4449174232772067364)
XLA Ops:
  0.0 5.3 %green.1 = bf16[4,128,128]{2,1,0:T(8,128)(2,1)} custom-call(bf16[1,1152,1152]{2,1,0:T(8,128)(2,1)} %m_hbm.1, s32[1,1152]{1,0:T(1,128)} %site_hbm.1, s32[1,1152]{1,0:T(1,128)} %time_hbm.1, s32[1,1152]{1,0:T(1,128)} %spin_hbm.1, f32[2,128]{1,0:T(2,128)} %free_hbm.1), custom_call_target="tpu_custom_call" | custom-call | tf_op jit(solution)/shard_map/green/pallas_call | solution.py:266
  5.3 15.7 %all_gather.3.own_ref = bf16[16,128,128]{2,1,0:T(8,128)(2,1)S(1)} all-gather(bf16[4,128,128]{2,1,0:T(8,128)(2,1)} %green.1), channel_id=1, replica_groups=mesh['y'=8,'z_lo'=4,'z_hi'=2,'x'=4,'core'=2] {'x'}, dimensions={0}, use_global_device_ids=true | all-gather | bytes 655360 | tf_op jit(solution)/shard_map/all_gather | solution.py:283
  21.0 1.9 %collective-permute-start = (bf16[16,128,128]{2,1,0:T(8,128)(2,1)S(1)}, bf16[16,128,128]{2,1,0:T(8,128)(2,1)S(1)}, u32[]{:S(2)}, u32[]{:S(2)}) collective-permute-start(bf16[16,128,128]{2,1,0:T(8,128)(2,1)S(1)} %all_gather.3.own_ref), channel_id=1, source_target_pairs={{0,1},{1,0},{2,3},{3,2},{4,5},{5,4},{6,7},{7,6},{8,9},{9,8},{10,11... | collective-permute-start | bytes 1572872 | tf_op jit(solution)/shard_map/ppermute | solution.py:284
  23.0 1.9 %collective-permute-done.other_ref = bf16[16,128,128]{2,1,0:T(8,128)(2,1)S(1)} collective-permute-done((bf16[16,128,128]{2,1,0:T(8,128)(2,1)S(1)}, bf16[16,128,128]{2,1,0:T(8,128)(2,1)S(1)}, u32[]{:S(2)}, u32[]{:S(2)}) %collective-permute-start) | collective-permute-done | bytes 524320 | tf_op jit(solution)/shard_map/ppermute | solution.py:284
  24.8 0.0 copy-start
  24.8 0.8 copy-done
  25.7 10.7 %pairs.1 = bf16[4096,128]{1,0:T(8,128)(2,1)S(1)} custom-call(s32[1]{0:T(128)} %bitcast.near_ref, bf16[16,128,128]{2,1,0:T(8,128)(2,1)S(1)} %all_gather.3.own_ref, bf16[16,128,128]{2,1,0:T(8,128)(2,1)S(1)} %collective-permute-done.other_ref, s32[128,128]{1,0:T(8,128)S(1)} %copy-done), custom_call_target="tpu_custom_call" | custom-call | tf_op jit(solution)/shard_map/pairs/pallas_call | solution.py:286
  36.3 46.4 %all_to_all.5.parts_ref = bf16[64,64,128]{2,1,0:T(8,128)(2,1)} all-to-all(bf16[64,64,128]{2,1,0:T(8,128)(2,1)S(1)} %bitcast.3), channel_id=1, replica_groups=mesh['y'=8,'z_lo'=4,'z_hi'=2,'x'=4,'core'=2] {'y','z_lo','z_hi'}, dimensions={0} | all-to-all | bytes 2097152 | tf_op jit(solution)/shard_map/all_to_all | solution.py:307
  82.7 2.1 %last.1 = f32[2,4,8,128]{3,2,1,0:T(8,128)} custom-call(bf16[64,64,128]{2,1,0:T(8,128)(2,1)} %all_to_all.5.parts_ref, s32[4,128]{1,0:T(4,128)} %cross_ref.1), custom_call_target="tpu_custom_call" | custom-call | tf_op jit(solution)/shard_map/last/pallas_call | solution.py:310
Async XLA Ops:
  21.0 3.8 %collective-permute-start = (bf16[16,128,128]{2,1,0:T(8,128)(2,1)S(1)}, bf16[16,128,128]{2,1,0:T(8,128)(2,1)S(1)}, u32[]{:S(2)}, u32[]{:S(2)}) collective-permute-start(bf16[16,128,128]{2,1,0:T(8,128)(2,1)S(1)} %all_gather.3.own_ref), channel_id=1, source_target_pairs={{0,1},{1,0},{2,3},{3,2},{4,5},{5,4},{6,7},{7,6},{8,9},{9,8},{10,11... | collective-permute-start | bytes 1572872 | tf_op jit(solution)/shard_map/ppermute | solution.py:284
  24.8 0.8 copy-start

commit v4 on v3

--- a/solution.py
+++ b/solution.py
@@ -262,7 +262,7 @@
 
 
 def body(vertex_matrix, vertex_site, vertex_time, vertex_spin, free_green, plus_table, cross_table):
-    limit = pltpu.CompilerParams(vmem_limit_bytes=48 << 20)
+    limit = pltpu.CompilerParams(vmem_limit_bytes=40 << 20)
     green = pl.pallas_call(
         green_kernel,
         out_shape=jax.ShapeDtypeStruct((4, W, W), BF16),
@@ -312,6 +312,7 @@
         out_shape=jax.ShapeDtypeStruct((2, 4, BROWS, W), F32),
         in_specs=[VMEM] * 2,
         out_specs=VMEM,
+        compiler_params=pltpu.CompilerParams(vmem_limit_bytes=4 << 20),
         name="last",
     )(parts, cross_table)
     return jnp.swapaxes(crossed, 2, 3)

time: 85.1 us -> 83.8 us (0.985)
  Pallas kernels: 18 us -> 16.8 us
    pallas_call x1, Pallas kernels: 2.08 us -> 0.86 us  [body(): pl.pallas_call(last_kernel, out_shape=jax.ShapeDtypeStruct((2, 4, BROWS,...]
where the time goes in v4:
time: 83.8 us; the launch traced here: 83.5 us
  blocking collectives  62 us (74%)
  Pallas kernels  16.8 us (20%)
  starting transfers between devices  1.91 us (2%)
  waiting for transfers between devices  1.87 us (2%)
  local copies, waits for them, and re-layouts  0.85 us (1%)
    all_to_all x1, blocking collectives, body(): lax.all_to_all(partial.reshape(64, 64, W), ('y', 'z_lo', 'z_hi'), 0, 0, t...  46.3 us
    all_gather x1, blocking collectives, body(): own = lax.all_gather(green, 'x', axis=0, tiled=True)  15.7 us
    pallas_call x1, Pallas kernels, body(): pl.pallas_call(pair_kernel, out_shape=jax.ShapeDtypeStruct((64 * 64, W),...  10.7 us
    pallas_call x1, Pallas kernels, body(): pl.pallas_call(green_kernel, out_shape=jax.ShapeDtypeStruct((4, W, W), BF...  5.32 us
    ppermute x1, starting transfers between devices, body(): other = lax.ppermute(own, 'core', [(0, 1), (1, 0)])  1.91 us
    ppermute x1, waiting for transfers between devices, body(): other = lax.ppermute(own, 'core', [(0, 1), (1, 0)])  1.87 us
  transfers between devices with their start and end apart: 1, of which 1 were waited for; matrix products, arithmetic and copies ran while one was open for 0% of the time, Pallas kernels for 0%

profile of v4, /device:TPU:2, one launch (start us, length us, event | category | flops | bytes accessed | tf_op | source)
XLA Modules:
  0.0 83.5 jit_solution(16360934742015296315)
XLA Ops:
  0.0 5.3 %green.1 = bf16[4,128,128]{2,1,0:T(8,128)(2,1)} custom-call(bf16[1,1152,1152]{2,1,0:T(8,128)(2,1)} %m_hbm.1, s32[1,1152]{1,0:T(1,128)} %site_hbm.1, s32[1,1152]{1,0:T(1,128)} %time_hbm.1, s32[1,1152]{1,0:T(1,128)} %spin_hbm.1, f32[2,128]{1,0:T(2,128)} %free_hbm.1), custom_call_target="tpu_custom_call" | custom-call | tf_op jit(solution)/shard_map/green/pallas_call | solution.py:266
  5.3 0.0 copy-start.1
  5.3 15.7 %all_gather.3.own_ref = bf16[16,128,128]{2,1,0:T(8,128)(2,1)S(1)} all-gather(bf16[4,128,128]{2,1,0:T(8,128)(2,1)} %green.1), channel_id=1, replica_groups=mesh['y'=8,'z_lo'=4,'z_hi'=2,'x'=4,'core'=2] {'x'}, dimensions={0}, use_global_device_ids=true | all-gather | bytes 655360 | tf_op jit(solution)/shard_map/all_gather | solution.py:283
  21.1 1.9 %collective-permute-start = (bf16[16,128,128]{2,1,0:T(8,128)(2,1)S(1)}, bf16[16,128,128]{2,1,0:T(8,128)(2,1)S(1)}, u32[]{:S(2)}, u32[]{:S(2)}) collective-permute-start(bf16[16,128,128]{2,1,0:T(8,128)(2,1)S(1)} %all_gather.3.own_ref), channel_id=1, source_target_pairs={{0,1},{1,0},{2,3},{3,2},{4,5},{5,4},{6,7},{7,6},{8,9},{9,8},{10,11... | collective-permute-start | bytes 1572872 | tf_op jit(solution)/shard_map/ppermute | solution.py:284
  23.0 1.9 %collective-permute-done.other_ref = bf16[16,128,128]{2,1,0:T(8,128)(2,1)S(1)} collective-permute-done((bf16[16,128,128]{2,1,0:T(8,128)(2,1)S(1)}, bf16[16,128,128]{2,1,0:T(8,128)(2,1)S(1)}, u32[]{:S(2)}, u32[]{:S(2)}) %collective-permute-start) | collective-permute-done | bytes 524320 | tf_op jit(solution)/shard_map/ppermute | solution.py:284
  24.9 0.0 copy-start
  24.9 0.8 %copy-done = s32[128,128]{1,0:T(8,128)S(1)} copy-done((s32[128,128]{1,0:T(8,128)S(1)}, s32[128,128]{1,0:T(8,128)}, u32[]{:S(2)}) %copy-start) | copy-done | bytes 65560
  25.7 10.7 %pairs.1 = bf16[4096,128]{1,0:T(8,128)(2,1)S(1)} custom-call(s32[1]{0:T(128)} %bitcast.near_ref, bf16[16,128,128]{2,1,0:T(8,128)(2,1)S(1)} %all_gather.3.own_ref, bf16[16,128,128]{2,1,0:T(8,128)(2,1)S(1)} %collective-permute-done.other_ref, s32[128,128]{1,0:T(8,128)S(1)} %copy-done), custom_call_target="tpu_custom_call" | custom-call | tf_op jit(solution)/shard_map/pairs/pallas_call | solution.py:286
  36.4 46.3 %all_to_all.5.parts_ref = bf16[64,64,128]{2,1,0:T(8,128)(2,1)S(1)} all-to-all(bf16[64,64,128]{2,1,0:T(8,128)(2,1)S(1)} %bitcast.3), channel_id=1, replica_groups=mesh['y'=8,'z_lo'=4,'z_hi'=2,'x'=4,'core'=2] {'y','z_lo','z_hi'}, dimensions={0} | all-to-all | bytes 2097152 | tf_op jit(solution)/shard_map/all_to_all | solution.py:307
  82.7 0.0 copy-done.1
  82.7 0.9 %last.1 = f32[2,4,8,128]{3,2,1,0:T(8,128)} custom-call(bf16[64,64,128]{2,1,0:T(8,128)(2,1)S(1)} %all_to_all.5.parts_ref, s32[4,128]{1,0:T(4,128)S(1)} %copy-done.1), custom_call_target="tpu_custom_call" | custom-call | tf_op jit(solution)/shard_map/last/pallas_call | solution.py:310
Async XLA Ops:
  5.3 77.3 %copy-start.1 = (s32[4,128]{1,0:T(4,128)S(1)}, s32[4,128]{1,0:T(4,128)}, u32[]{:S(2)}) copy-start(s32[4,128]{1,0:T(4,128)} %cross_ref.1) | copy-start | bytes 6148
  21.1 3.8 %collective-permute-start = (bf16[16,128,128]{2,1,0:T(8,128)(2,1)S(1)}, bf16[16,128,128]{2,1,0:T(8,128)(2,1)S(1)}, u32[]{:S(2)}, u32[]{:S(2)}) collective-permute-start(bf16[16,128,128]{2,1,0:T(8,128)(2,1)S(1)} %all_gather.3.own_ref), channel_id=1, source_target_pairs={{0,1},{1,0},{2,3},{3,2},{4,5},{5,4},{6,7},{7,6},{8,9},{9,8},{10,11... | collective-permute-start | bytes 1572872 | tf_op jit(solution)/shard_map/ppermute | solution.py:284
  24.9 0.8 %copy-start = (s32[128,128]{1,0:T(8,128)S(1)}, s32[128,128]{1,0:T(8,128)}, u32[]{:S(2)}) copy-start(s32[128,128]{1,0:T(8,128)} %plus_ref.1) | copy-start | bytes 196612

commit v5 on v4

--- a/solution.py
+++ b/solution.py
@@ -81,11 +81,11 @@
     for c in range(NV // PIECE):
         large[c].wait()
         piece = m_ref[:, c * PIECE : (c + 1) * PIECE]
+        projected = jnp.dot(rows_ref[...], piece, preferred_element_type=F32).astype(BF16)
         for s in range(2):
             mine = slice(2 * W * s, 2 * W * (s + 1))
-            projected = jnp.dot(rows_ref[mine, :], piece, preferred_element_type=F32)
             term = lax.dot_general(
-                projected.astype(BF16),
+                projected[mine],
                 rows_ref[mine, c * PIECE : (c + 1) * PIECE],
                 (((1,), (1,)), ((), ())),
                 preferred_element_type=F32,
@@ -100,40 +100,26 @@
         out_ref[2 * s + 1] = (-(hr * fi + hi * fr) * norm_factor).astype(BF16)
 
 
-def pair_kernel(
-    near_ref, own_ref, other_ref, plus_ref, out_ref,
-    both_ref, pick_ref, lead_ref, trail_ref, spread_ref, col_ref, even_ref, odd_ref,
-    sums_ref, straight_ref, turn_ref,
-):
-    def plane(w, s, part):
-        ref = own_ref if w < 4 else other_ref
-        return ref[(w % 4) * 4 + 2 * s + part]
-
-    near = near_ref[0]
-    plus_t = plus_ref[...].astype(F32).T.astype(jnp.int32)
-    lane = lax.broadcasted_iota(jnp.int32, (W, W), 1)
+def tables(near, plus):
+    plus_t = plus.astype(F32).T.astype(jnp.int32)
     slot = lax.broadcasted_iota(jnp.int32, (16, W), 0)
     point = lax.broadcasted_iota(jnp.int32, (16, W), 1)
     owned = (slot // 8) * 64 + near * 8 + slot % 8
     chosen = (point == owned).astype(BF16)
     plus_own = jnp.dot(chosen, plus_t.astype(F32).astype(BF16), preferred_element_type=F32)
+    return plus_t, chosen, plus_own
+
+
+def take_walkers(plane_ref, first, plus_t, chosen, plus_own, both_ref, lead_ref, trail_ref, col_ref):
     plus_own_i = plus_own.astype(jnp.int32)
-    plus_col = plus_own.T.astype(jnp.int32)
-    for b in range(16):
-        hot = (plus_col[:, b : b + 1] == lane).astype(F32).astype(BF16)
-        pick_ref[b * W : (b + 1) * W, 0:W] = hot
-        pick_ref[b * W : (b + 1) * W, W : 2 * W] = hot
+    lane = lax.broadcasted_iota(jnp.int32, (W, W), 1)
     eye = (lax.broadcasted_iota(jnp.int32, (W, W), 0) == lane).astype(F32).astype(BF16)
-
-    def fetch(group, w, dst):
-        picks = pick_ref[group * 4 * W : (group + 1) * 4 * W, :]
-        dst[w] = jnp.dot(picks, both_ref[w], preferred_element_type=F32)
-
-    for w in range(NEAR):
+    for local in range(4):
+        w = first + local
         for part in range(2):
             total = None
             for s in range(2):
-                value = plane(w, s, part)
+                value = plane_ref[local * 4 + 2 * s + part]
                 both_ref[w, s * W : (s + 1) * W, part * W : (part + 1) * W] = value
                 k = (w * 2 + s) * 2 + part
                 lead = jnp.take_along_axis(value.astype(F32), plus_t, axis=1).astype(BF16)
@@ -148,6 +134,38 @@
                 )
                 total = columns if total is None else total + columns
             col_ref[w * 2 + part] = total
+
+
+def own_kernel(near_ref, own_ref, plus_ref, both_ref, pick_ref, lead_ref, trail_ref, col_ref):
+    plus_t, chosen, plus_own = tables(near_ref[0], plus_ref[...])
+    lane = lax.broadcasted_iota(jnp.int32, (W, W), 1)
+    plus_col = plus_own.T.astype(jnp.int32)
+    for b in range(16):
+        hot = (plus_col[:, b : b + 1] == lane).astype(F32).astype(BF16)
+        pick_ref[b * W : (b + 1) * W, 0:W] = hot
+        pick_ref[b * W : (b + 1) * W, W : 2 * W] = hot
+    trail_ref[...] = jnp.zeros_like(trail_ref)
+    take_walkers(own_ref, 0, plus_t, chosen, plus_own, both_ref, lead_ref, trail_ref, col_ref)
+
+
+def pair_kernel(
+    near_ref, other_ref, plus_ref, both_own, pick_ref, lead_own, trail_own, col_own, out_ref,
+    both_ref, lead_ref, trail_ref, spread_ref, col_ref, even_ref, odd_ref,
+    sums_ref, straight_ref, turn_ref,
+):
+    def fetch(group, w, dst):
+        picks = pick_ref[group * 4 * W : (group + 1) * 4 * W, :]
+        dst[w] = jnp.dot(picks, both_ref[w], preferred_element_type=F32)
+
+    both_ref[0:4] = both_own[...]
+    lead_ref[0 : 16 * PITCH, :] = lead_own[...]
+    trail_ref[...] = trail_own[...]
+    col_ref[0:8] = col_own[...]
+    for w in range(4):
+        fetch(0, w, even_ref)
+    plus_t, chosen, plus_own = tables(near_ref[0], plus_ref[...])
+    take_walkers(other_ref, 4, plus_t, chosen, plus_own, both_ref, lead_ref, trail_ref, col_ref)
+    for w in range(4, NEAR):
         fetch(0, w, even_ref)
 
     planes = 4 * NEAR
@@ -207,8 +225,8 @@
                     mine = pl.ds(pl.multiple_of(j * W + start, 8), 8)
                     re = im = None
                     for v in range(NEAR):
-                        row_r = col_ref[2 * v, pl.ds(b, 8, stride=0), :]
-                        row_i = col_ref[2 * v + 1, pl.ds(b, 8, stride=0), :]
+                        row_r = col_ref[2 * v, b : b + 1, :]
+                        row_i = col_ref[2 * v + 1, b : b + 1, :]
                         yr = jnp.take_along_axis(now[v, mine, 0:W], index, axis=1)
                         yi = jnp.take_along_axis(now[v, mine, W : 2 * W], index, axis=1)
                         add_r, add_i = row_r * yr - row_i * yi, row_r * yi + row_i * yr
@@ -283,14 +301,29 @@
     own = lax.all_gather(green, "x", axis=0, tiled=True)
     other = lax.ppermute(own, "core", [(0, 1), (1, 0)])
     near = (lax.axis_index("x") * 2 + lax.axis_index("core")).reshape(1)
+    half = (
+        jax.ShapeDtypeStruct((4, 2 * W, 2 * W), BF16),
+        jax.ShapeDtypeStruct((16 * W, 2 * W), BF16),
+        jax.ShapeDtypeStruct((16 * PITCH, W), F32),
+        jax.ShapeDtypeStruct((16 * STEP, W), F32),
+        jax.ShapeDtypeStruct((8, 16, W), F32),
+    )
+    halves = pl.pallas_call(
+        own_kernel,
+        out_shape=half,
+        in_specs=[SMEM] + [VMEM] * 2,
+        out_specs=(VMEM,) * 5,
+        compiler_params=pltpu.CompilerParams(vmem_limit_bytes=16 << 20),
+        cost_estimate=pl.CostEstimate(flops=2 << 30, bytes_accessed=8 << 20, transcendentals=0),
+        name="own",
+    )(near, own, plus_table)
     partial = pl.pallas_call(
         pair_kernel,
         out_shape=jax.ShapeDtypeStruct((64 * 64, W), BF16),
-        in_specs=[SMEM] + [VMEM] * 3,
+        in_specs=[SMEM] + [VMEM] * 7,
         out_specs=VMEM,
         scratch_shapes=[
             pltpu.VMEM((NEAR, 2 * W, 2 * W), BF16),
-            pltpu.VMEM((16 * W, 2 * W), BF16),
             pltpu.VMEM((4 * NEAR * PITCH, W), F32),
             pltpu.VMEM((16 * STEP, W), F32),
             pltpu.VMEM((16 * W, 16 * 4 * NEAR), F32),
@@ -303,7 +336,7 @@
         ],
         compiler_params=limit,
         name="pairs",
-    )(near, own, other, plus_table)
+    )(near, other, plus_table, *halves)
     parts = lax.all_to_all(
         partial.reshape(64, 64, W), ("y", "z_lo", "z_hi"), 0, 0, tiled=True
     )

time: 83.8 us -> 82.9 us (0.989)
  waiting for transfers between devices: 1.87 us -> 0.01 us
    ppermute x1, waiting for transfers between devices: 1.87 us -> 0.01 us  [body(): other = lax.ppermute(own, 'core', [(0, 1), (1, 0)])]
    pallas_call x0 -> x1, Pallas kernels: none -> 1.55 us  [body(): pl.pallas_call(own_kernel, out_shape=half, in_specs=[SMEM] + [VMEM] * 2,...]
  transfers between devices with their start and end apart: 1 -> 1, of which waited for: 1 -> 0; matrix products, arithmetic and copies ran while one was open for 0% -> 0% of each run, Pallas kernels for 0% -> 2%
where the time goes in v5:
time: 82.9 us; the launch traced here: 82.7 us
  blocking collectives  62.5 us (75%)
  Pallas kernels  17.3 us (21%)
  starting transfers between devices  1.91 us (2%)
  local copies, waits for them, and re-layouts  0.84 us (1%)
    all_to_all x1, blocking collectives, body(): lax.all_to_all(partial.reshape(64, 64, W), ('y', 'z_lo', 'z_hi'), 0, 0, t...  46.8 us
    all_gather x1, blocking collectives, body(): own = lax.all_gather(green, 'x', axis=0, tiled=True)  15.7 us
    pallas_call x1, Pallas kernels, body(): pl.pallas_call(pair_kernel, out_shape=jax.ShapeDtypeStruct((64 * 64, W),...  9.93 us
    pallas_call x1, Pallas kernels, body(): pl.pallas_call(green_kernel, out_shape=jax.ShapeDtypeStruct((4, W, W), BF...  5 us
    ppermute x1, starting transfers between devices, body(): other = lax.ppermute(own, 'core', [(0, 1), (1, 0)])  1.91 us
  transfers between devices with their start and end apart: 1, of which 0 were waited for; matrix products, arithmetic and copies ran while one was open for 0% of the time, Pallas kernels for 2%

profile of v5, /device:TPU:2, one launch (start us, length us, event | category | flops | bytes accessed | tf_op | source)
XLA Modules:
  0.0 82.7 jit_solution(8317180401561787183)
XLA Ops:
  0.0 5.0 %green.1 = bf16[4,128,128]{2,1,0:T(8,128)(2,1)} custom-call(bf16[1,1152,1152]{2,1,0:T(8,128)(2,1)} %m_hbm.1, s32[1,1152]{1,0:T(1,128)} %site_hbm.1, s32[1,1152]{1,0:T(1,128)} %time_hbm.1, s32[1,1152]{1,0:T(1,128)} %spin_hbm.1, f32[2,128]{1,0:T(2,128)} %free_hbm.1), custom_call_target="tpu_custom_call" | custom-call | tf_op jit(solution)/shard_map/green/pallas_call | solution.py:284
  5.0 15.7 %all_gather.3.own_ref = bf16[16,128,128]{2,1,0:T(8,128)(2,1)S(1)} all-gather(bf16[4,128,128]{2,1,0:T(8,128)(2,1)} %green.1), channel_id=1, replica_groups=mesh['y'=8,'z_lo'=4,'z_hi'=2,'x'=4,'core'=2] {'x'}, dimensions={0}, use_global_device_ids=true | all-gather | bytes 655360 | tf_op jit(solution)/shard_map/all_gather | solution.py:301
  20.7 1.9 %collective-permute-start = (bf16[16,128,128]{2,1,0:T(8,128)(2,1)S(1)}, bf16[16,128,128]{2,1,0:T(8,128)(2,1)S(1)}, u32[]{:S(2)}, u32[]{:S(2)}) collective-permute-start(bf16[16,128,128]{2,1,0:T(8,128)(2,1)S(1)} %all_gather.3.own_ref), channel_id=1, source_target_pairs={{0,1},{1,0},{2,3},{3,2},{4,5},{5,4},{6,7},{7,6},{8,9},{9,8},{10,11... | collective-permute-start | bytes 1572872 | tf_op jit(solution)/shard_map/ppermute | solution.py:302
  22.7 0.0 copy-start
  22.7 0.8 %copy-done = s32[128,128]{1,0:T(8,128)S(1)} copy-done((s32[128,128]{1,0:T(8,128)S(1)}, s32[128,128]{1,0:T(8,128)}, u32[]{:S(2)}) %copy-start) | copy-done | bytes 65560
  23.5 0.0 copy-start.1
  23.5 1.5 %own.1 = (bf16[4,256,256]{2,1,0:T(8,128)(2,1)S(1)}, bf16[2048,256]{1,0:T(8,128)(2,1)S(1)}, f32[2064,128]{1,0:T(8,128)S(1)}, f32[528,128]{1,0:T(8,128)S(1)}, f32[8,16,128]{2,1,0:T(8,128)S(1)}) custom-call(s32[1]{0:T(128)} %bitcast.near_ref, bf16[16,128,128]{2,1,0:T(8,128)(2,1)S(1)} %all_gather.3.own_ref, s32[128,128]{1,0:T(8,128)S(1)} %copy-done), custom_call_target="tpu_custom_call" | custom-call | flops 2147483648 | bytes 8388608 | tf_op jit(solution)/shard_map/own/pallas_call | solution.py:311
  25.1 0.0 collective-permute-done.other_ref
  25.1 0.0 copy-done.1
  25.1 0.0 copy-start.2
  25.1 9.9 %pairs.1 = bf16[4096,128]{1,0:T(8,128)(2,1)S(1)} custom-call(s32[1]{0:T(128)} %bitcast.near_ref, bf16[16,128,128]{2,1,0:T(8,128)(2,1)S(1)} %collective-permute-done.other_ref, s32[128,128]{1,0:T(8,128)S(1)} %copy-done.1, bf16[4,256,256]{2,1,0:T(8,128)(2,1)S(1)} %get-tuple-element.10.both_own, bf16[2048,256]{1,0:T(8,128)(2,1)S(1)} %get-tuple-element.11.pick_ref, ...), custom_call_target="tpu_custom_call" | custom-call | tf_op jit(solution)/shard_map/pairs/pallas_call | solution.py:320
  35.0 46.8 %all_to_all.5.parts_ref = bf16[64,64,128]{2,1,0:T(8,128)(2,1)S(1)} all-to-all(bf16[64,64,128]{2,1,0:T(8,128)(2,1)S(1)} %bitcast.3), channel_id=1, replica_groups=mesh['y'=8,'z_lo'=4,'z_hi'=2,'x'=4,'core'=2] {'y','z_lo','z_hi'}, dimensions={0} | all-to-all | bytes 2097152 | tf_op jit(solution)/shard_map/all_to_all | solution.py:340
  81.8 0.0 copy-done.2
  81.8 0.9 %last.1 = f32[2,4,8,128]{3,2,1,0:T(8,128)} custom-call(bf16[64,64,128]{2,1,0:T(8,128)(2,1)S(1)} %all_to_all.5.parts_ref, s32[4,128]{1,0:T(4,128)S(1)} %copy-done.2), custom_call_target="tpu_custom_call" | custom-call | tf_op jit(solution)/shard_map/last/pallas_call | solution.py:343
Async XLA Ops:
  20.7 4.3 %collective-permute-start = (bf16[16,128,128]{2,1,0:T(8,128)(2,1)S(1)}, bf16[16,128,128]{2,1,0:T(8,128)(2,1)S(1)}, u32[]{:S(2)}, u32[]{:S(2)}) collective-permute-start(bf16[16,128,128]{2,1,0:T(8,128)(2,1)S(1)} %all_gather.3.own_ref), channel_id=1, source_target_pairs={{0,1},{1,0},{2,3},{3,2},{4,5},{5,4},{6,7},{7,6},{8,9},{9,8},{10,11... | collective-permute-start | bytes 1572872 | tf_op jit(solution)/shard_map/ppermute | solution.py:302
  22.7 0.8 %copy-start = (s32[128,128]{1,0:T(8,128)S(1)}, s32[128,128]{1,0:T(8,128)}, u32[]{:S(2)}) copy-start(s32[128,128]{1,0:T(8,128)} %plus_ref.3) | copy-start | bytes 196612
  23.5 1.6 %copy-start.1 = (s32[128,128]{1,0:T(8,128)S(1)}, s32[128,128]{1,0:T(8,128)}, u32[]{:S(2)}) copy-start(s32[128,128]{1,0:T(8,128)} %plus_ref.3) | copy-start | bytes 196612
  25.1 56.7 %copy-start.2 = (s32[4,128]{1,0:T(4,128)S(1)}, s32[4,128]{1,0:T(4,128)}, u32[]{:S(2)}) copy-start(s32[4,128]{1,0:T(4,128)} %cross_ref.1) | copy-start | bytes 6148
